TPU v7x, 32 devices: a whole 2x2x4 slice. The times are simulated.
32 devices in a mesh: dp: 8 (over z, x), tensor: 4 (over y, core).
Axes of the slice: x: 2, y: 2, z: 4, core: 2. Of those that a mesh axis runs over, the one named last changes fastest.
Arguments:
- tokens: bfloat16 [4096, 768], P(('dp', 'tensor')), may hold values from -6 to 6
- place: int32 [8, 512], P('dp'), may hold values from 0 to 511, each once within a row
- lengths: int32 [8, 3], P('dp'), may hold values from 1 to 320, 512 in all within a row
- expert_ids: int32 [2, 4096, 2], P(None, 'dp'), may hold values from 0 to 3, all different within a row
- gate_values: float32 [2, 4096, 2], P(None, 'dp'), may hold values from 0.25 to 1
- cotangent: bfloat16 [4096, 768], P(('dp', 'tensor')), may hold values from -6 to 6
- gain_attn: float32 [2, 768], P(None, 'dp'), may hold values from 0.5 to 1.5
- w_query: float32 [2, 768, 768], P(None, 'dp', 'tensor'), may hold values from -0.21875 to 0.21875
- w_key: float32 [2, 768, 768], P(None, 'dp', 'tensor'), may hold values from -0.21875 to 0.21875
- w_value: float32 [2, 768, 768], P(None, 'dp', 'tensor'), may hold values from -0.21875 to 0.21875
- w_out: float32 [2, 768, 768], P(None, 'tensor', 'dp'), may hold values from -0.75 to 0.75
- gain_ffn: float32 [2, 768], P(None, 'dp'), may hold values from 0.5 to 1.5
- exp_gate: float32 [2, 4, 768, 2048], P(None, None, 'dp', 'tensor'), may hold values from -0.21875 to 0.21875
- exp_up: float32 [2, 4, 768, 2048], P(None, None, 'dp', 'tensor'), may hold values from -0.21875 to 0.21875
- exp_down: float32 [2, 4, 2048, 768], P(None, None, 'tensor', 'dp'), may hold values from -0.1875 to 0.1875
- dense_gate: float32 [2, 768, 2048], P(None, 'dp', 'tensor'), may hold values from -0.21875 to 0.21875
- dense_up: float32 [2, 768, 2048], P(None, 'dp', 'tensor'), may hold values from -0.21875 to 0.21875
- dense_down: float32 [2, 2048, 768], P(None, 'tensor', 'dp'), may hold values from -0.125 to 0.125
Outputs:
- mixed: bfloat16 [4096, 768], P(('dp', 'tensor'))
- input_grad: float32 [4096, 768], P(('dp', 'tensor'))
- grad_gain_attn: float32 [2, 768], P(None, 'dp')
- grad_query: float32 [2, 768, 768], P(None, 'dp', 'tensor')
- grad_key: float32 [2, 768, 768], P(None, 'dp', 'tensor')
- grad_value: float32 [2, 768, 768], P(None, 'dp', 'tensor')
- grad_out: float32 [2, 768, 768], P(None, 'tensor', 'dp')
- grad_gain_ffn: float32 [2, 768], P(None, 'dp')
- grad_exp_gate: float32 [2, 4, 768, 2048], P(None, None, 'dp', 'tensor')
- grad_exp_up: float32 [2, 4, 768, 2048], P(None, None, 'dp', 'tensor')
- grad_exp_down: float32 [2, 4, 2048, 768], P(None, None, 'tensor', 'dp')
- grad_dense_gate: float32 [2, 768, 2048], P(None, 'dp', 'tensor')
- grad_dense_up: float32 [2, 768, 2048], P(None, 'dp', 'tensor')
- grad_dense_down: float32 [2, 2048, 768], P(None, 'tensor', 'dp')
Inputs may be any that keep to these rules, and one draw needn't show every extreme that they name: `place`: each row is a permutation of 0 .. 511. `lengths`: each row sums to 512; its largest entry is exactly 320. `expert_ids`: a token's 2 experts differ; every expert is used by some token of each layer.
All inputs are finite; a program needn't handle non-finite values.
Results may differ from a plain program's by a relative error of at most 0.03.
Values may be sent and summed in bfloat16 or wider, within the bound.
A program may use at most 192 MiB of HBM per device.

v0:
```python
import functools

import jax
import jax.numpy as jnp
import numpy as np
from jax import lax
from jax.experimental import pallas as pl
from jax.experimental.pallas import tpu as pltpu
from jax.sharding import PartitionSpec as P

HD = 64
EPSILON = 1e-06
MASKED_SCORE = -1e30
MESH = pl.DeviceIdType.MESH
ANY = pl.BlockSpec(memory_space=pl.ANY)
VMEM = pl.BlockSpec(memory_space=pltpu.VMEM)
F32 = jnp.float32
BF16 = jnp.bfloat16
PARTS = 2
BOTH, OUTER, INNER = range(3)


def split_dp(dp):
    inner = 2 ** ((dp.bit_length() - 1) // 2)
    return dp // inner, inner


def place_of(inner):
    d = lax.axis_index("dp")
    return lax.div(d, inner), lax.rem(d, inner), lax.axis_index("tensor")


def across(t):
    return lax.rem(t + 2, 4), t + 1 - 2 * lax.rem(t, 2)


def meet(devices):
    barrier = pltpu.get_barrier_semaphore()
    for device in devices:
        pl.semaphore_signal(barrier, inc=1, device_id=device, device_id_type=MESH)
    pl.semaphore_wait(barrier, len(devices))


def send(source, target, send_sem, recv_sem, device):
    copy = pltpu.make_async_remote_copy(
        src_ref=source,
        dst_ref=target,
        send_sem=send_sem,
        recv_sem=recv_sem,
        device_id=device,
        device_id_type=MESH,
    )
    copy.start()
    return copy


def gather_kernel(dp, own, out, *sems):
    take = Gather(1, dp, out, sems)
    out[0, take.t] = own[...]
    meet(take.friends())
    take.start()
    take.complete(0)
    take.finish()


def gather(own, dp, ident):
    return pl.pallas_call(
        functools.partial(gather_kernel, dp),
        out_shape=jax.ShapeDtypeStruct((1, 4) + own.shape, own.dtype),
        in_specs=[VMEM],
        out_specs=VMEM,
        scratch_shapes=gather_sems(1),
        compiler_params=pltpu.CompilerParams(collective_id=ident, has_side_effects=True),
        name="gather",
    )(own)


def fetch_kernel(outer, inner, count, *refs):
    cut = Cut(refs)
    extra = Fetch(outer, inner, cut(count), cut(count), cut(count), cut(5), [BOTH] * count)
    meet(extra.zdev[1:] + extra.xdev)
    extra.start()
    extra.settle()
    for turn in extra.turns():
        turn()
    extra.finish()


def fetch(owns, outer, inner, ident):
    count = len(owns)
    return pl.pallas_call(
        functools.partial(fetch_kernel, outer, inner, count),
        out_shape=fetch_outs(owns, outer, inner, [BOTH] * count),
        in_specs=[ANY] * count,
        out_specs=[ANY] * count,
        scratch_shapes=fetch_scratch(owns, outer, inner, [BOTH] * count),
        compiler_params=pltpu.CompilerParams(collective_id=ident, has_side_effects=True),
        name="fetch",
    )(*owns)


def push_kernel(outer, inner, count, *refs):
    cut = Cut(refs)
    extra = Push(outer, inner, cut(count), cut(count), cut(3 * count), cut(6))
    meet(extra.zdev[:-1] + extra.xdev)
    extra.start()
    for turn in extra.turns():
        turn()
    extra.finish()


def push(parts, outer, inner, ident):
    count = len(parts)
    return pl.pallas_call(
        functools.partial(push_kernel, outer, inner, count),
        out_shape=push_outs(parts, outer),
        in_specs=[ANY] * count,
        out_specs=[ANY] * count,
        scratch_shapes=push_scratch(parts, outer, inner),
        compiler_params=pltpu.CompilerParams(collective_id=ident, has_side_effects=True),
        name="push",
    )(*parts)


def nearest(index, size, step):
    table = [sorted(range(size), key=lambda other: (abs(other - at), other)) for at in range(size)]
    found = 0
    for at in range(size):
        found = found + jnp.where(index == at, table[at][step], 0)
    return found


class Gather:
    def __init__(self, outer, inner, table, sems, parts=1):
        self.outer, self.inner, self.table, self.parts = outer, inner, table, parts
        self.zs, self.zr, self.ys, self.yr, self.cs, self.cr = sems
        self.dz, self.dx, self.t = place_of(inner)
        self.d = lax.axis_index("dp")
        self.size = table.shape[2] // parts
        ty, tc = across(self.t)
        self.ty = ty
        self.pair, self.core = (self.d, ty), (self.d, tc)
        self.source = [nearest(self.dz, outer, step) for step in range(outer)]
        self.zdev = [(source * inner + self.dx, self.t) for source in self.source]
        self.steps = outer * parts
        self.yc, self.cc, self.dc = [], [], []

    def friends(self):
        return self.zdev[1:] + [self.pair, self.core]

    def rows(self, step):
        return pl.ds(step % self.parts * self.size, self.size)

    def origin(self, step):
        return self.source[step // self.parts]

    def outward(self, step, target, sent):
        at = self.origin(step) * self.parts + step % self.parts
        block = self.table.at[self.origin(step), self.t, self.rows(step)]
        target = jnp.minimum(jnp.maximum(target, 0), self.outer - 1)
        return pltpu.make_async_remote_copy(
            src_ref=block,
            dst_ref=block,
            send_sem=self.zs.at[at if sent is None else sent],
            recv_sem=self.zr.at[at],
            device_id=(target * self.inner + self.dx, self.t),
            device_id_type=MESH,
        )

    def passes(self, step):
        if self.outer == 1:
            return []
        if step < self.parts:
            last = self.steps + step
            return [
                (self.dz < self.outer - 1, self.outward(step, self.dz + 1, None)),
                (self.dz > 0, self.outward(step, self.dz - 1, last)),
            ]
        ahead = jnp.where(self.origin(step) < self.dz, self.dz + 1, self.dz - 1)
        inside = (ahead >= 0) & (ahead < self.outer)
        return [(inside, self.outward(step, ahead, None))]

    def start(self):
        for step in range(self.parts):
            for inside, copy in self.passes(step):
                pl.when(inside)(copy.start)
        for step in range(self.parts):
            self.forward(step)

    def arrive(self, step):
        self.outward(step, self.dz, None).wait_recv()
        for inside, copy in self.passes(step):
            pl.when(inside)(copy.start)
        self.forward(step)

    def forward(self, step):
        block = self.table.at[self.origin(step), self.t, self.rows(step)]
        self.yc.append(send(block, block, self.ys.at[step], self.yr.at[step], self.pair))
        self.cc.append(send(block, block, self.cs.at[step], self.cr.at[step], self.core))

    def complete(self, step):
        self.yc[step].wait_recv()
        at = self.steps + step
        block = self.table.at[self.origin(step), self.ty, self.rows(step)]
        self.dc.append(send(block, block, self.cs.at[at], self.cr.at[at], self.core))
        self.cc[step].wait_recv()
        self.dc[step].wait_recv()

    def finish(self):
        for step in range(self.steps):
            for inside, copy in self.passes(step):
                pl.when(inside)(copy.wait_send)
        for copy in self.yc + self.cc + self.dc:
            copy.wait_send()


class Scatter:
    def __init__(self, outer, inner, part, room, sems, parts=1):
        self.outer, self.part, self.parts = outer, part, parts
        self.from_c, self.sum_c, self.from_y, self.sum_y, self.from_z = room
        self.cs, self.cr, self.ys, self.yr, self.zs, self.zr = sems
        dz, dx, t = place_of(inner)
        d = lax.axis_index("dp")
        ty, tc = across(t)
        self.size = part.shape[3] // parts
        self.dz, self.y, self.c = dz, lax.div(t, 2), lax.rem(t, 2)
        self.pair, self.core = (d, ty), (d, tc)
        self.source = [nearest(dz, outer, step) for step in range(outer)]
        self.zdev = [(source * inner + dx, t) for source in self.source]
        self.steps = outer * parts
        self.cc, self.yc, self.zc = {}, {}, {}

    def rows(self, step):
        return pl.ds(step % self.parts * self.size, self.size)

    def core_send(self, step):
        source = self.source[step // self.parts]
        self.cc[step] = send(
            self.part.at[source, :, 1 - self.c, self.rows(step)],
            self.from_c.at[step],
            self.cs.at[step],
            self.cr.at[step],
            self.core,
        )

    def pair_send(self, step):
        source = self.source[step // self.parts]
        self.cc[step].wait_recv()
        mine = self.part[source, :, self.c, self.rows(step)].astype(F32)
        self.sum_c[step] = (mine + self.from_c[step].astype(F32)).astype(BF16)
        self.yc[step] = send(
            self.sum_c.at[step, 1 - self.y],
            self.from_y.at[step],
            self.ys.at[step],
            self.yr.at[step],
            self.pair,
        )

    def summed(self, step):
        self.yc[step].wait_recv()
        return self.sum_c[step, self.y].astype(F32) + self.from_y[step].astype(F32)

    def outward(self, step, source, away):
        at = (away - 1) * self.parts + step % self.parts
        return pltpu.make_async_remote_copy(
            src_ref=source,
            dst_ref=self.from_z.at[at],
            send_sem=self.zs.at[at],
            recv_sem=self.zr.at[at],
            device_id=self.zdev[step // self.parts],
            device_id_type=MESH,
        )

    def outer_send(self, step):
        self.sum_y[step] = self.summed(step).astype(BF16)
        away = lax.rem(self.source[step // self.parts] - self.dz + self.outer, self.outer)
        self.zc[step] = self.outward(step, self.sum_y.at[step], away)
        self.zc[step].start()

    def total(self):
        pieces = []
        for piece in range(self.parts):
            total = self.summed(piece)
            for step in range(self.parts + piece, self.steps, self.parts):
                away = lax.rem(self.dz - self.source[step // self.parts] + self.outer, self.outer)
                self.outward(step, self.sum_y.at[step], away).wait_recv()
                at = (away - 1) * self.parts + piece
                total = total + self.from_z[at].astype(F32)
            pieces.append(total)
        return pieces[0] if self.parts == 1 else jnp.concatenate(pieces, axis=0)

    def finish(self):
        for group in (self.cc, self.yc, self.zc):
            for step in group:
                group[step].wait_send()


def gather_sems(outer, parts=1):
    dma = pltpu.SemaphoreType.DMA
    steps = outer * parts
    return [dma((steps + parts,))] + [dma((steps,)) for _ in range(3)] + [dma((2 * steps,))] * 2


def scatter_sems(outer, parts=1):
    dma = pltpu.SemaphoreType.DMA
    return [dma((outer * parts,)) for _ in range(6)]


def scatter_room(outer, rows, width, parts=1):
    steps, size = outer * parts, rows // parts
    return [
        pltpu.VMEM((steps, 2, size, width), BF16),
        pltpu.VMEM((steps, 2, size, width), BF16),
        pltpu.VMEM((steps, size, width), BF16),
        pltpu.VMEM((steps, size, width), BF16),
        pltpu.VMEM((max(steps - parts, 1), size, width), BF16),
    ]


def pipeline(take, give, compute, begin, after, middle, late):
    steps, parts = take.steps, take.parts
    middle, late = list(middle), list(late)
    lag = parts + 1
    take.start()
    begin()
    for step in range(steps):
        if step + parts < steps:
            take.arrive(step + parts)
        if step + parts == steps - 1:
            after()
        take.complete(step)
        compute(step)
        give.core_send(step)
        if step:
            give.pair_send(step - 1)
        if step - lag >= parts:
            give.outer_send(step - lag)
        if step + parts >= steps and middle:
            middle.pop(0)()
    sent = max(parts, steps - lag)
    late = middle + late
    share = max(1, (len(late) + lag) // (lag + 1))
    give.pair_send(steps - 1)
    for step in range(sent, steps):
        for _ in range(share):
            if late:
                late.pop(0)()
        give.outer_send(step)
    for work in late:
        work()


class Fetch:
    def __init__(self, outer, inner, owns, outs, holds, sems, modes):
        self.outer, self.inner, self.owns, self.outs, self.holds = outer, inner, owns, outs, holds
        self.zs, self.zr, self.xs, self.xr, self.ls = sems
        self.modes = modes
        self.dz, dx, t = place_of(inner)
        self.dx, self.d = dx, lax.axis_index("dp")
        self.source = [nearest(self.dz, outer, step) for step in range(outer)]
        self.zdev = [(source * inner + dx, t) for source in self.source]
        self.xdev = [(self.dz * inner + lax.rem(dx + j, inner), t) for j in range(1, inner)]
        self.zc, self.xc, self.into, self.back = [], {}, {}, {}

    def own(self, i, where):
        return self.owns[i].at[where if self.owns[i].shape[0] == self.outer else 0]

    def slot(self, i, source):
        if self.modes[i] == OUTER:
            return self.outs[i].at[source]
        return self.outs[i].at[source * self.inner + self.dx]

    def copy(self, i, step, source, target):
        away = lax.rem(source + self.outer, self.outer)
        at = i * self.outer + away
        return pltpu.make_async_remote_copy(
            src_ref=target[0],
            dst_ref=target[1],
            send_sem=self.zs.at[at],
            recv_sem=self.zr.at[at],
            device_id=self.zdev[step],
            device_id_type=MESH,
        )

    def start(self, first=0, last=None, aside=True):
        for i in range(first, len(self.owns) if last is None else last):
            inner = self.modes[i] == INNER
            here = self.owns[i] if inner else self.own(i, self.dz)
            at = i * (self.outer + 1)
            self.into[i] = pltpu.make_async_copy(here, self.holds[i], self.ls.at[at])
            self.into[i].start()
            if inner:
                for step, source in enumerate(self.source):
                    self.spread(i, step, self.owns[i].at[source], self.slot(i, source))
                continue
            for step in range(1, self.outer):
                source = self.source[step]
                refs = (self.own(i, source), self.slot(i, self.dz))
                self.zc.append(self.copy(i, step, source - self.dz, refs))
                self.zc[-1].start()
            if aside:
                self.aside(i)

    def aside(self, i):
        if self.modes[i] == BOTH:
            self.spread(i, 0, self.own(i, self.dz), self.slot(i, self.dz))

    def spread(self, i, step, block, target):
        for j in range(1, self.inner):
            at = (i * self.outer + step) * self.inner + j
            self.xc[i, step, j] = send(
                block, target, self.xs.at[at], self.xr.at[at], self.xdev[j - 1]
            )

    def settle(self):
        for i, into in self.into.items():
            into.wait()
            at = i * (self.outer + 1)
            if self.modes[i] == INNER:
                pairs = [
                    (self.holds[i].at[source], self.slot(i, source)) for source in self.source
                ]
            else:
                pairs = [(self.holds[i], self.slot(i, self.dz))]
            self.back[i] = [
                pltpu.make_async_copy(*pair, self.ls.at[at + 1 + k])
                for k, pair in enumerate(pairs)
            ]
            for copy in self.back[i]:
                copy.start()

    def turn(self, i, step):
        source = self.source[step]
        block = self.slot(i, source)
        self.copy(i, step, self.dz - source, (block, block)).wait_recv()
        if self.modes[i] == BOTH:
            self.spread(i, step, block, block)

    def turns(self, first=0, last=None):
        return [
            functools.partial(self.turn, i, step)
            for i in range(first, len(self.owns) if last is None else last)
            for step in range(1, self.outer)
            if self.modes[i] != INNER
        ]

    def land(self, i):
        for key in self.xc:
            if key[0] == i:
                self.xc[key].wait_recv()
        for copy in self.back[i]:
            copy.wait()

    def finish(self, first=0):
        for key in self.xc:
            if key[0] >= first:
                self.xc[key].wait_recv()
            self.xc[key].wait_send()
        for copy in self.zc:
            copy.wait_send()
        for i in self.back:
            if i >= first:
                for copy in self.back[i]:
                    copy.wait()


def fetch_outs(owns, outer, inner, modes):
    return [
        jax.ShapeDtypeStruct(
            (outer if mode == OUTER else outer * inner,) + own.shape[1:], own.dtype
        )
        for own, mode in zip(owns, modes)
    ]


def fetch_scratch(owns, outer, inner, modes):
    dma = pltpu.SemaphoreType.DMA
    count = max(len(owns), 1)
    return [
        pltpu.VMEM(own.shape if mode == INNER else own.shape[1:], own.dtype)
        for own, mode in zip(owns, modes)
    ] + [
        dma((count * outer,)),
        dma((count * outer,)),
        dma((count * outer * inner,)),
        dma((count * outer * inner,)),
        dma((count * (outer + 1),)),
    ]


class Push:
    def __init__(self, outer, inner, parts, outs, room, sems):
        count = len(parts)
        self.outer, self.inner, self.parts, self.outs = outer, inner, parts, outs
        self.froms, self.mine, self.sums = room[:count], room[count : 2 * count], room[2 * count :]
        self.xs, self.xr, self.zs, self.zr, self.ls, self.ks = sems
        self.dz, dx, t = place_of(inner)
        self.dx = dx
        near = [nearest(self.dz, outer, step) for step in range(outer)]
        self.source = near[:0:-1] + near[:1]
        self.zdev = [(source * inner + dx, t) for source in self.source]
        self.xdev = [(self.dz * inner + lax.rem(dx + j, inner), t) for j in range(1, inner)]
        self.xc, self.zc, self.loads, self.keeps = {}, [], {}, []

    def start(self, first=0, last=None):
        for i in range(first, len(self.parts) if last is None else last):
            for step, source in enumerate(self.source):
                for j in range(1, self.inner):
                    slot = source * self.inner + lax.rem(self.dx + j, self.inner)
                    at = (i * self.outer + step) * self.inner + j
                    self.xc[i, step, j] = send(
                        self.parts[i].at[slot],
                        self.froms[i].at[j - 1, step],
                        self.xs.at[at],
                        self.xr.at[at],
                        self.xdev[j - 1],
                    )
                self.loads[i, step] = pltpu.make_async_copy(
                    self.parts[i].at[source * self.inner + self.dx],
                    self.mine[i].at[step],
                    self.ls.at[i * self.outer + step],
                )
                self.loads[i, step].start()

    def turn(self, i, step):
        self.loads[i, step].wait()
        total = self.mine[i][step].astype(F32)
        for j in range(1, self.inner):
            self.xc[i, step, j].wait_recv()
            total = total + self.froms[i][j - 1, step].astype(F32)
        self.sums[i][step] = total.astype(self.sums[i].dtype)
        target = self.outs[i].at[self.dz]
        if step < self.outer - 1:
            away = lax.rem(self.source[step] - self.dz + self.outer, self.outer)
            at = i * self.outer + away
            self.zc.append(
                send(self.sums[i].at[step], target, self.zs.at[at], self.zr.at[at], self.zdev[step])
            )
        else:
            self.keeps.append(
                pltpu.make_async_copy(self.sums[i].at[step], target, self.ks.at[i])
            )
            self.keeps[-1].start()

    def turns(self):
        return [
            functools.partial(self.turn, i, step)
            for i in range(len(self.parts))
            for step in range(self.outer)
        ]

    def finish(self):
        for copy in self.zc:
            copy.wait_recv()
            copy.wait_send()
        for key in self.xc:
            self.xc[key].wait_send()
        for copy in self.keeps:
            copy.wait()


def push_outs(parts, outer):
    return [jax.ShapeDtypeStruct((outer,) + part.shape[1:], part.dtype) for part in parts]


def push_scratch(parts, outer, inner):
    dma = pltpu.SemaphoreType.DMA
    count = max(len(parts), 1)
    across_x = [pltpu.VMEM((inner - 1, outer) + part.shape[1:], part.dtype) for part in parts]
    own = [pltpu.VMEM((outer,) + part.shape[1:], part.dtype) for part in parts]
    return (
        across_x
        + own
        + own
        + [
            dma((count * outer * inner,)),
            dma((count * outer * inner,)),
            dma((count * outer,)),
            dma((count * outer,)),
            dma((count * outer,)),
            dma((count,)),
        ]
    )


class Cut:
    def __init__(self, refs):
        self.refs, self.at = refs, 0

    def __call__(self, count):
        self.at += count
        return self.refs[self.at - count : self.at]


class Mixer:
    def __init__(self, outer, inner, table, lines, mix, sems):
        self.lines, self.mix = lines, mix
        dx = lax.rem(lax.axis_index("dp"), inner)
        self.loads = [
            pltpu.make_async_copy(table.at[at * inner + dx], lines.at[at], sems.at[at])
            for at in range(outer)
        ]
        for load in self.loads:
            load.start()

    def turn(self):
        for at, load in enumerate(self.loads):
            load.wait()
            self.mix[at] = jnp.transpose(self.lines[at]).reshape(self.mix.shape[1:])


def ffn_forward_kernel(outer, inner, kinds, modes, level, row, *refs):
    count = len(modes)
    cut = Cut(refs)
    resid, gain, mix_any, w_in_any, w_down_any = cut(5)
    owns = cut(count)
    out, b_out, gu_out = cut(3)
    fetched = cut(count)
    w_in, w_down, b, gu, part, mix_rows, mix = cut(7)
    room, take_sems, give_sems = cut(5), cut(6), cut(6)
    load_sem, keep_b, keep_gu, load_mix = cut(4)
    extra = Fetch(outer, inner, owns, fetched, cut(count), cut(5), modes) if count else None
    rows, width = resid.shape
    third = w_down.shape[1]
    slim = third // kinds
    loads = [
        pltpu.make_async_copy(w_in_any, w_in, load_sem.at[0]),
        pltpu.make_async_copy(w_down_any, w_down, load_sem.at[1]),
    ]
    for load in loads:
        load.start()
    take = Gather(outer, inner, b, take_sems, PARTS)
    give = Scatter(outer, inner, part, room, give_sems, PARTS)
    size = rows // PARTS
    mixer = Mixer(outer, inner, mix_any, mix_rows, mix, load_mix)
    x = resid[...]
    inverse = lax.rsqrt(jnp.mean(x * x, axis=-1, keepdims=True) + EPSILON)
    b[take.dz, take.t] = (x * inverse * gain[row : row + 1]).astype(BF16)
    meet(take.friends() + (extra.xdev if count else []))
    keeps = []

    def compute(step):
        source, q = take.origin(step), step % PARTS
        here = take.rows(step)
        if step == 0:
            for load in loads:
                load.wait()
        rows_in = b[source, :, here].reshape(4 * size, width)
        scale = mix[source, :, here].reshape(4 * size, mix.shape[-1])
        both = dot(rows_in, w_in[...])
        gu[source, q] = both.astype(BF16)
        gate, up = both[:, :third], both[:, third:]
        hidden = gate * jax.nn.sigmoid(gate) * up
        pieces = []
        for e in range(kinds):
            piece = hidden[:, e * slim : (e + 1) * slim]
            if e < kinds - 1:
                at = level * (kinds - 1) + e
                piece = piece * scale[:, at : at + 1]
            pieces.append(piece.astype(BF16))
        hidden = jnp.concatenate(pieces, axis=1)
        sent = dot_nt(hidden, w_down[...]).astype(BF16)
        part[source, :, :, here] = sent.reshape(2, 2, size, width)
        if q == PARTS - 1:
            at = step // PARTS
            keeps.append(pltpu.make_async_copy(b.at[source], b_out.at[source], keep_b.at[at]))
            keeps.append(pltpu.make_async_copy(gu.at[source], gu_out.at[source], keep_gu.at[at]))
            keeps[-1].start()
            keeps[-2].start()

    def after():
        if count:
            extra.start()
            extra.settle()

    pipeline(take, give, compute, mixer.turn, after, extra.turns() if count else [], [])
    out[...] = resid[...] + give.total()
    take.finish()
    give.finish()
    if count:
        extra.finish()
    for keep in keeps:
        keep.wait()


def ffn_forward(
    resid, gain, level, row, kinds, mix, w_in, w_down, owns, modes, outer, inner, ident
):
    dma = pltpu.SemaphoreType.DMA
    rows, width = resid.shape
    third = w_down.shape[1]
    count = len(owns)
    return pl.pallas_call(
        functools.partial(ffn_forward_kernel, outer, inner, kinds, modes, level, row),
        out_shape=[
            jax.ShapeDtypeStruct((rows, width), F32),
            jax.ShapeDtypeStruct((outer, 4, rows, width), BF16),
            jax.ShapeDtypeStruct((outer, PARTS, 4 * rows // PARTS, 2 * third), BF16),
        ]
        + fetch_outs(owns, outer, inner, modes),
        in_specs=[VMEM, VMEM, ANY, ANY, ANY] + [ANY] * count,
        out_specs=[VMEM, ANY, ANY] + [ANY] * count,
        scratch_shapes=[
            pltpu.VMEM(w_in.shape, BF16),
            pltpu.VMEM(w_down.shape, BF16),
            pltpu.VMEM((outer, 4, rows, width), BF16),
            pltpu.VMEM((outer, PARTS, 4 * rows // PARTS, 2 * third), BF16),
            pltpu.VMEM((outer, 2, 2, rows, width), BF16),
            pltpu.VMEM((outer,) + mix.shape[1:], F32),
            pltpu.VMEM((outer, 4, rows, mix.shape[1]), F32),
        ]
        + scatter_room(outer, rows, width, PARTS)
        + gather_sems(outer, PARTS)
        + scatter_sems(outer, PARTS)
        + [dma((2,)), dma((outer,)), dma((outer,)), dma((outer,))]
        + (fetch_scratch(owns, outer, inner, modes) if count else []),
        compiler_params=pltpu.CompilerParams(
            collective_id=ident, has_side_effects=True, vmem_limit_bytes=62 << 20
        ),
        name="ffn_forward",
    )(resid, gain, mix, w_in, w_down, *owns)


def ffn_backward_kernel(outer, inner, kinds, count, level, row, *refs):
    cut = Cut(refs)
    grad_y, resid, gain, mix_any, w_in_any, w_down_any, b_any, gu_any = cut(8)
    parts = cut(count)
    out, gain_out, grad_in, grad_down = cut(4)
    pushed = cut(count)
    w_in, w_down, b, gb, gu, dgu, hid, flip, part, mix_rows, mix = cut(11)
    room, take_sems, give_sems = cut(5), cut(6), cut(6)
    load_sem, load_gu, load_mix = cut(3)
    extra = Push(outer, inner, parts, pushed, cut(3 * count), cut(6)) if count else None
    rows, width = resid.shape
    tall = outer * 4 * rows
    third = w_down.shape[1]
    slim = third // kinds
    loads = [
        pltpu.make_async_copy(source, target, load_sem.at[i])
        for i, (source, target) in enumerate(
            ((b_any, b), (w_down_any, w_down), (w_in_any, w_in))
        )
    ]
    for load in loads:
        load.start()
    take = Gather(outer, inner, gb, take_sems, PARTS)
    give = Scatter(outer, inner, part, room, give_sems, PARTS)
    size = rows // PARTS
    mixer = Mixer(outer, inner, mix_any, mix_rows, mix, load_mix)
    fills = [
        pltpu.make_async_copy(gu_any.at[source], gu.at[source], load_gu.at[step])
        for step, source in enumerate(take.source)
    ]
    for fill in fills:
        fill.start()
    gb[take.dz, take.t] = grad_y[...].astype(BF16)
    meet(take.friends() + (extra.xdev if count else []))

    def compute(step):
        source, q = take.origin(step), step % PARTS
        here = take.rows(step)
        if step == 0:
            loads[1].wait()
            loads[2].wait()
        if q == 0:
            fills[step // PARTS].wait()
        rows_in = gb[source, :, here].reshape(4 * size, width)
        mixed = mix[source, :, here].reshape(4 * size, mix.shape[-1])
        grad_hidden = dot(rows_in, w_down[...])
        both = gu[source, q].astype(F32)
        gate, up = both[:, :third], both[:, third:]
        sigma = jax.nn.sigmoid(gate)
        act = gate * sigma
        slope = sigma * (1.0 + gate * (1.0 - sigma))
        hidden, grad_gate, grad_up = act * up, grad_hidden * up * slope, grad_hidden * act
        for e in range(kinds):
            cols = slice(e * slim, (e + 1) * slim)
            more = slice(third + e * slim, third + (e + 1) * slim)
            at = level * (kinds - 1) + e
            scale = mixed[:, at : at + 1] if e < kinds - 1 else 1.0
            hid[source, q, :, cols] = (hidden[:, cols] * scale).astype(BF16)
            dgu[source, q, :, cols] = (grad_gate[:, cols] * scale).astype(BF16)
            dgu[source, q, :, more] = (grad_up[:, cols] * scale).astype(BF16)
        sent = dot_nt(dgu[source, q], w_in[...]).astype(BF16)
        part[source, :, :, here] = sent.reshape(2, 2, size, width)

    def turned(table):
        @pl.loop(0, outer)
        def _(source):
            for q in range(PARTS):
                block = table[source, :, q * size : (q + 1) * size].reshape(4 * size, width)
                at = pl.multiple_of((source * PARTS + q) * 4 * size, 4 * size)
                flip[:, pl.ds(at, 4 * size)] = jnp.transpose(block)

    def weigh(target, source, low, high):
        values = source[...].reshape(tall, source.shape[-1])

        @pl.loop(0, width // 256)
        def _(at):
            here = pl.ds(pl.multiple_of(at * 256, 256), 256)
            target[here, low:high] = dot(flip[here, :], values[:, low:high]).astype(BF16)

    def begin():
        if count:
            extra.start()
        mixer.turn()
        loads[0].wait()
        turned(b)

    def pieces(total):
        return [(low, min(low + 256, total)) for low in range(0, total, 256)]

    late = [functools.partial(weigh, grad_in, dgu, *span) for span in pieces(2 * third)]
    late += [functools.partial(turned, gb)]
    late += [functools.partial(weigh, grad_down, hid, *span) for span in pieces(third)]
    pipeline(take, give, compute, begin, lambda: None, extra.turns() if count else [], late)
    grad_b = give.total()
    x = resid[...]
    inverse = lax.rsqrt(jnp.mean(x * x, axis=-1, keepdims=True) + EPSILON)
    unit = x * inverse
    gain_out[...] = jnp.sum(grad_b * unit, axis=0, keepdims=True)
    out[...] = grad_y[...].astype(F32) + norm_back(grad_b, gain[row : row + 1], unit, inverse)
    take.finish()
    give.finish()
    if count:
        extra.finish()


def ffn_backward(
    grad_y, resid, gain, level, row, kinds, mix, w_in, w_down, b, both, parts, outer, inner, ident
):
    dma = pltpu.SemaphoreType.DMA
    rows, width = resid.shape
    third = w_down.shape[1]
    count = len(parts)
    return pl.pallas_call(
        functools.partial(ffn_backward_kernel, outer, inner, kinds, count, level, row),
        out_shape=[
            jax.ShapeDtypeStruct((rows, width), F32),
            jax.ShapeDtypeStruct((1, width), F32),
            jax.ShapeDtypeStruct((width, 2 * third), BF16),
            jax.ShapeDtypeStruct((width, third), BF16),
        ]
        + push_outs(parts, outer),
        in_specs=[VMEM, VMEM, VMEM, ANY, ANY, ANY, ANY, ANY] + [ANY] * count,
        out_specs=[VMEM, VMEM, VMEM, VMEM] + [ANY] * count,
        scratch_shapes=[
            pltpu.VMEM(w_in.shape, BF16),
            pltpu.VMEM(w_down.shape, BF16),
            pltpu.VMEM((outer, 4, rows, width), BF16),
            pltpu.VMEM((outer, 4, rows, width), BF16),
            pltpu.VMEM((outer, PARTS, 4 * rows // PARTS, 2 * third), BF16),
            pltpu.VMEM((outer, PARTS, 4 * rows // PARTS, 2 * third), BF16),
            pltpu.VMEM((outer, PARTS, 4 * rows // PARTS, third), BF16),
            pltpu.VMEM((width, outer * 4 * rows), BF16),
            pltpu.VMEM((outer, 2, 2, rows, width), BF16),
            pltpu.VMEM((outer,) + mix.shape[1:], F32),
            pltpu.VMEM((outer, 4, rows, mix.shape[1]), F32),
        ]
        + scatter_room(outer, rows, width, PARTS)
        + gather_sems(outer, PARTS)
        + scatter_sems(outer, PARTS)
        + [dma((3,)), dma((outer,)), dma((outer,))]
        + (push_scratch(parts, outer, inner) if count else []),
        compiler_params=pltpu.CompilerParams(
            collective_id=ident, has_side_effects=True, vmem_limit_bytes=63 << 20
        ),
        name="ffn_backward",
    )(grad_y, resid, gain, mix, w_in, w_down, b, both, *parts)


def swap_halves(values):
    width = values.shape[1]
    lane = lax.broadcasted_iota(jnp.int32, values.shape, 1)
    low = lax.rem(lane, HD) < HD // 2
    return jnp.where(
        low, pltpu.roll(values, width - HD // 2, 1), pltpu.roll(values, HD // 2, 1)
    )


def allowed_rows(marks, spot, top):
    del top
    return (spot >= marks[:, 1:2]) & (spot <= marks[:, 0:1])


def attn_forward_kernel(outer, inner, modes, lead, row, *refs):
    count = len(modes)
    dp = outer * inner
    cut = Cut(refs)
    x_in, tables, marks, spot = cut(4)
    gain, weight = (None, None) if lead else cut(2)
    owns = cut(count)
    out, a_out, qk_out, v_out, lse_out, att_out = cut(6)
    gain_out = cut(1)[0] if lead else None
    fetched = cut(count)
    w, a, qk, v, att, part = cut(6)
    room, take_sems, give_sems = cut(5), cut(6), cut(6)
    load_sem, keep_sem = cut(2)
    extra = Fetch(outer, inner, owns, fetched, cut(count), cut(5), modes)
    rows, width = x_in.shape
    heads_width = w.shape[1] // 4
    heads = heads_width // HD
    take = Gather(1, dp, a, take_sems)
    give = Scatter(1, dp, part, room, give_sems)
    x = x_in[...].astype(F32)
    inverse = lax.rsqrt(jnp.mean(x * x, axis=-1, keepdims=True) + EPSILON)
    friends = take.friends() + extra.zdev[1:] + extra.xdev
    if lead:
        (gains,) = cut(1)
        meet(friends)
        extra.start(0, 2)
        extra.start(2, None, False)
        extra.settle()
        for turn in extra.turns(0, 1):
            turn()
        extra.land(0)
        load = pltpu.make_async_copy(fetched[0], gains, load_sem.at[0])
        load.start()
        load.wait()
        gain_out[...] = jnp.sum(gains[...], axis=0)
        a[0, take.t] = (x * inverse * gain_out[row : row + 1]).astype(BF16)
        turns = extra.turns(1, 2)
        turns[0]()
        take.start()
        for turn in turns[1:]:
            turn()
        for i in range(2, count):
            extra.aside(i)
        extra.land(1)
        slot = fetched[1].shape[1]
        loads = [
            pltpu.make_async_copy(
                fetched[1].at[at], w.at[pl.ds(at * slot, slot)], load_sem.at[at]
            )
            for at in range(dp)
        ]
        for load in loads:
            load.start()
        for load in loads:
            load.wait()
    else:
        load = pltpu.make_async_copy(weight, w, load_sem.at[0])
        load.start()
        a[0, take.t] = (x * inverse * gain[row : row + 1]).astype(BF16)
        meet(friends)
        take.start()
        extra.start()
        extra.settle()
        load.wait()
    done = 2 if lead else 0
    turns = extra.turns(done)

    def project(block):
        both = dot(a[0, block], w[:, : 3 * heads_width])
        raw = both[:, : 2 * heads_width]
        times = 2 * heads_width // tables.shape[-1]
        cosine = jnp.concatenate([tables[0, block]] * times, axis=1)
        sine = jnp.concatenate([tables[1, block]] * times, axis=1)
        qk[block] = (raw * cosine + swap_halves(raw) * sine).astype(BF16)
        v[block] = both[:, 2 * heads_width :].astype(BF16)

    project(take.t)
    take.complete(0)
    for other in range(1, 4):
        project(lax.rem(take.t + other, 4))
    keeps = [pltpu.make_async_copy(a.at[0], a_out, keep_sem.at[0])]
    keeps.append(pltpu.make_async_copy(qk, qk_out, keep_sem.at[1]))
    keeps.append(pltpu.make_async_copy(v, v_out, keep_sem.at[2]))
    for keep in keeps:
        keep.start()

    def attend(block):
        keys = qk[...].reshape(4 * rows, 2 * heads_width)
        values = v[...].reshape(4 * rows, heads_width)
        allowed = allowed_rows(marks[block], spot[...], 0)
        pieces = []
        for head in range(heads):
            here = slice(head * HD, (head + 1) * HD)
            there = slice(heads_width + head * HD, heads_width + (head + 1) * HD)
            scores = dot_nt(qk[block, :, here], keys[:, there])
            scores = jnp.where(allowed, scores * HD ** (-0.5), MASKED_SCORE)
            top = jnp.max(scores, axis=-1, keepdims=True)
            expo = jnp.exp(scores - top)
            total = jnp.sum(expo, axis=-1, keepdims=True)
            probs = (expo / total).astype(BF16)
            lse_out[block, :, head : head + 1] = top + jnp.log(total)
            pieces.append(dot(probs, values[:, here]).astype(BF16))
        att[block] = jnp.concatenate(pieces, axis=1)
        sent = dot_nt(att[block], w[:, 3 * heads_width :]).astype(BF16)
        part[0, lax.div(block, 2), lax.rem(block, 2)] = sent

    y, c = give.y, give.c
    attend(2 * (1 - y) + 1 - c)
    attend(2 * y + 1 - c)
    give.core_send(0)
    turns[0]()
    attend(2 * (1 - y) + c)
    attend(2 * y + c)
    give.pair_send(0)
    for turn in turns[1:]:
        turn()
    keeps.append(pltpu.make_async_copy(att, att_out, keep_sem.at[3]))
    keeps[-1].start()
    out[...] = x_in[...].astype(F32) + give.total()
    take.finish()
    give.finish()
    extra.finish(done)
    for keep in keeps:
        keep.wait()


def attn_forward(
    x, gain, row, weight, tables, marks, spot, owns, modes, outer, inner, ident
):
    count = len(owns)
    dma = pltpu.SemaphoreType.DMA
    rows, width = x.shape
    lead = weight is None
    shape = (width, owns[1].shape[-1]) if lead else weight.shape
    slim = shape[1] // 4
    extras = [] if lead else [gain, weight]
    kept = [(4, rows, width), (4, rows, 2 * slim), (4, rows, slim)]
    return pl.pallas_call(
        functools.partial(attn_forward_kernel, outer, inner, modes, lead, row),
        out_shape=[jax.ShapeDtypeStruct((rows, width), F32)]
        + [jax.ShapeDtypeStruct(shape, BF16) for shape in kept]
        + [
            jax.ShapeDtypeStruct((4, rows, 8), F32),
            jax.ShapeDtypeStruct((4, rows, slim), BF16),
        ]
        + ([jax.ShapeDtypeStruct((8, width), F32)] if lead else [])
        + fetch_outs(owns, outer, inner, modes),
        in_specs=[VMEM] * 4 + ([] if lead else [VMEM, ANY]) + [ANY] * count,
        out_specs=[VMEM, ANY, ANY, ANY, VMEM, ANY] + [VMEM] * lead + [ANY] * count,
        scratch_shapes=[
            pltpu.VMEM(shape, BF16),
            pltpu.VMEM((1, 4, rows, width), BF16),
            pltpu.VMEM(kept[1], BF16),
            pltpu.VMEM(kept[2], BF16),
            pltpu.VMEM(kept[2], BF16),
            pltpu.VMEM((1, 2, 2, rows, width), BF16),
        ]
        + scatter_room(1, rows, width)
        + gather_sems(1)
        + scatter_sems(1)
        + [dma((outer * inner,)), dma((4,))]
        + fetch_scratch(owns, outer, inner, modes)
        + ([pltpu.VMEM((outer * inner,) + owns[0].shape[1:], F32)] if lead else []),
        compiler_params=pltpu.CompilerParams(collective_id=ident, has_side_effects=True),
        name="attn_forward",
    )(x, tables, marks, spot, *extras, *owns)


def attn_backward_kernel(outer, inner, count, last, row, *refs):
    dp = outer * inner
    cut = Cut(refs)
    grad_in, x_in, gain, weight, tables, marks, spot = cut(7)
    a_in, qk_in, v_in, lse, att_in = cut(5)
    others = cut(last)
    parts = cut(count)
    out, gain_out = cut(2)
    (grad_w,) = (None,) if last else cut(1)
    total = count + 1 if last else count
    pushed = cut(total)
    w, a, qk, v, att, ga, g_att, raw, part = cut(9)
    room, take_sems, give_sems = cut(5), cut(6), cut(6)
    (load_sem,) = cut(1)
    room_x, sems_x = cut(3 * total), cut(6)
    if last:
        held, from_t, from_d, ts, tr, ds, dr = cut(7)
        parts = tuple(parts) + (held,)
    extra = Push(outer, inner, parts, pushed, room_x, sems_x)
    turns = extra.turns()
    friends = []
    rows, width = x_in.shape
    tall = 4 * rows
    heads_width = w.shape[1] // 4
    heads = heads_width // HD
    loads = [
        pltpu.make_async_copy(source, target, load_sem.at[i])
        for i, (source, target) in enumerate(
            ((weight, w), (qk_in, qk), (v_in, v), (att_in, att), (a_in, a))
        )
    ]
    for load in loads:
        load.start()
    take = Gather(1, dp, ga, take_sems)
    give = Scatter(1, dp, part, room, give_sems)
    ga[0, take.t] = grad_in[...].astype(BF16)
    if last:
        team = [(take.d, lax.rem(take.t + k, 4)) for k in range(1, 4)]
        peers = [(lax.rem(take.d + k, dp), take.t) for k in range(1, dp)]
        friends = team + peers
    else:
        friends = take.friends() + extra.zdev[:-1] + extra.xdev
    meet(friends)
    take.start()
    extra.start(0, count)
    for load in loads:
        load.wait()
    take.complete(0)
    turns[0]()
    grads = ga[...].reshape(tall, width)
    g_att[...] = dot(grads, w[:, 3 * heads_width :]).astype(BF16)
    all_qk = qk[...].reshape(tall, 2 * heads_width)
    all_v = v[...].reshape(tall, heads_width)
    all_marks = marks[...].reshape(tall, marks.shape[-1])
    all_lse = lse[...].reshape(tall, lse.shape[-1])
    allowed = allowed_rows(all_marks, spot[...], 0)
    q_grads, k_grads, v_grads = [], [], []
    for head in range(heads):
        here = slice(head * HD, (head + 1) * HD)
        there = slice(heads_width + head * HD, heads_width + (head + 1) * HD)
        query, key = all_qk[:, here], all_qk[:, there]
        scores = dot_nt(query, key)
        scores = jnp.where(allowed, scores * HD ** (-0.5), MASKED_SCORE)
        probs = jnp.exp(scores - all_lse[:, head : head + 1])
        grad_probs = dot_nt(g_att[:, here], all_v[:, here])
        inner = jnp.sum(grad_probs * probs, axis=-1, keepdims=True)
        grad_scores = (probs * (grad_probs - inner)).astype(BF16)
        v_grads.append(dot_tn(probs.astype(BF16), g_att[:, here]).astype(BF16))
        q_grads.append(dot(grad_scores, key))
        k_grads.append(dot_tn(grad_scores, query))
    rotated = jnp.concatenate(q_grads + k_grads, axis=1) * HD ** (-0.5)
    times = 2 * heads_width // tables.shape[-1]
    cosine = jnp.concatenate([tables[0].reshape(tall, -1)] * times, axis=1)
    sine = jnp.concatenate([tables[1].reshape(tall, -1)] * times, axis=1)
    raw[:, : 2 * heads_width] = (rotated * cosine - swap_halves(rotated) * sine).astype(BF16)
    raw[:, 2 * heads_width :] = jnp.concatenate(v_grads, axis=1)
    def back(block):
        at = pl.ds(pl.multiple_of(block * rows, rows), rows)
        sent = dot_nt(raw[at, :], w[:, : 3 * heads_width]).astype(BF16)
        part[0, lax.div(block, 2), lax.rem(block, 2)] = sent

    turns[1]()
    y, c = give.y, give.c
    back(2 * (1 - y) + 1 - c)
    back(2 * y + 1 - c)
    give.core_send(0)
    back(2 * (1 - y) + c)
    back(2 * y + c)
    give.pair_send(0)
    turns[2]()
    grad_raw = dot_tn(a[...].reshape(tall, width), raw[...]).astype(BF16)
    grad_out = dot_tn(grads, att[...].reshape(tall, heads_width)).astype(BF16)
    if last:
        held[:, :, : 3 * heads_width] = grad_raw.reshape(dp, width // dp, -1)
        held[:, :, 3 * heads_width :] = grad_out.reshape(dp, width // dp, -1)
    else:
        grad_w[:, : 3 * heads_width] = grad_raw
        grad_w[:, 3 * heads_width :] = grad_out
    grad_a = give.total()
    x = x_in[...].astype(F32)
    inverse = lax.rsqrt(jnp.mean(x * x, axis=-1, keepdims=True) + EPSILON)
    unit = x * inverse
    part_gain = jnp.sum(grad_a * unit, axis=0, keepdims=True)
    if last:
        from_t[take.t] = jnp.zeros(from_t.shape[1:], F32)
        from_t[take.t, row : row + 1] = part_gain
        for at, other in zip([at for at in range(last + 1) if at != row], others):
            from_t[take.t, at : at + 1] = other[...]
    else:
        gain_out[...] = part_gain
    out[...] = grad_in[...] + norm_back(grad_a, gain[row : row + 1], unit, inverse)
    if last:
        extra.start(count, total)
        mine = from_t.at[take.t]
        copies = [
            send(mine, mine, ts.at[k], tr.at[k], device) for k, device in enumerate(team)
        ]
        for copy in copies:
            copy.wait_recv()
        from_d[take.d] = jnp.sum(from_t[...], axis=0)
        turns[3]()
        mine = from_d.at[take.d]
        more = [send(mine, mine, ds.at[k], dr.at[k], device) for k, device in enumerate(peers)]
        for turn in turns[4:]:
            turn()
        for copy in more:
            copy.wait_recv()
        gain_out[...] = jnp.sum(from_d[...], axis=0)
        for copy in copies + more:
            copy.wait_send()
    else:
        for turn in turns[3:]:
            turn()
    take.finish()
    give.finish()
    extra.finish()


def attn_backward(
    grad, x, gain, row, weight, tables, marks, spot, kept, others, parts, outer, inner, ident
):
    count = len(parts)
    dma = pltpu.SemaphoreType.DMA
    rows, width = x.shape
    slim = weight.shape[1] // 4
    dp = outer * inner
    last = len(others)
    whole = jax.ShapeDtypeStruct((dp, width // dp, 4 * slim), BF16)
    moved = list(parts) + ([whole] if last else [])
    wide = (8, width) if last else (1, width)
    return pl.pallas_call(
        functools.partial(attn_backward_kernel, outer, inner, count, last, row),
        out_shape=[
            jax.ShapeDtypeStruct((rows, width), F32),
            jax.ShapeDtypeStruct(wide, F32),
        ]
        + ([] if last else [jax.ShapeDtypeStruct(weight.shape, BF16)])
        + push_outs(moved, outer),
        in_specs=[VMEM, VMEM, VMEM, ANY, VMEM, VMEM, VMEM, ANY, ANY, ANY, VMEM, ANY]
        + [VMEM] * last
        + [ANY] * count,
        out_specs=[VMEM, VMEM] + ([] if last else [VMEM]) + [ANY] * len(moved),
        scratch_shapes=[
            pltpu.VMEM(weight.shape, BF16),
            pltpu.VMEM((4, rows, width), BF16),
            pltpu.VMEM((4, rows, 2 * slim), BF16),
            pltpu.VMEM((4, rows, slim), BF16),
            pltpu.VMEM((4, rows, slim), BF16),
            pltpu.VMEM((1, 4, rows, width), BF16),
            pltpu.VMEM((4 * rows, slim), BF16),
            pltpu.VMEM((4 * rows, 3 * slim), BF16),
            pltpu.VMEM((1, 2, 2, rows, width), BF16),
        ]
        + scatter_room(1, rows, width)
        + gather_sems(1)
        + scatter_sems(1)
        + [dma((5,))]
        + push_scratch(moved, outer, inner)
        + (
            [
                pltpu.VMEM(whole.shape, BF16),
                pltpu.VMEM((4, 8, width), F32),
                pltpu.VMEM((dp, 8, width), F32),
                dma((3,)),
                dma((3,)),
                dma((dp,)),
                dma((dp,)),
            ]
            if last
            else []
        ),
        compiler_params=pltpu.CompilerParams(
            collective_id=ident, has_side_effects=True, vmem_limit_bytes=62 << 20
        ),
        name="attn_backward",
    )(grad, x, gain, weight, tables, marks, spot, *kept, *others, *parts)


def pack_kernel(outer, dp, *refs):
    cut = Cut(refs)
    place, lengths, freqs, ids, gates, gain_attn, gain_ffn = cut(7)
    attn_any, ffn_any = cut(4), cut(6)
    tables, marks, spot, gains, mix = cut(5)
    layers, rows = gain_attn.shape
    attn_out, in_out, down_out = cut(layers), cut(layers), cut(layers)
    attn_in, ffn_in = cut(4), cut(6)
    attn_held, in_held, down_held = cut(layers), cut(layers), cut(layers)
    load_attn, load_ffn, keep = cut(3)
    loads_attn = [
        pltpu.make_async_copy(source, target, load_attn.at[i])
        for i, (source, target) in enumerate(zip(attn_any, attn_in))
    ]
    loads_ffn = [
        [
            pltpu.make_async_copy(source.at[level], target.at[level], load_ffn.at[level, i])
            for i, (source, target) in enumerate(zip(ffn_any, ffn_in))
        ]
        for level in range(layers)
    ]
    for load in sum(loads_ffn, loads_attn):
        load.start()
    count = place.shape[1]
    where = place[...]
    begins, end = jnp.zeros_like(where), 0
    for doc in range(lengths.shape[1]):
        end = end + lengths[0, doc]
        begins = begins + jnp.where(where >= end, lengths[0, doc], 0)
    spot[...] = where.astype(F32)
    lines = jnp.concatenate([where.astype(F32), begins.astype(F32)] * 4, axis=0)
    marks[...] = jnp.transpose(lines).reshape(4, count // 4, 8)
    angles = (where - begins).astype(F32) * freqs[...]
    cosine, sine = jnp.cos(angles), jnp.sin(angles)
    tables[0] = jnp.transpose(jnp.concatenate([cosine] * 4, axis=0)).reshape(4, count // 4, 128)
    tables[1] = jnp.transpose(jnp.concatenate([-sine, sine, -sine, sine], axis=0)).reshape(
        4, count // 4, 128
    )
    experts = mix.shape[0] // layers
    for level in range(layers):
        for e in range(experts):
            row = jnp.zeros((1, count), F32)
            for slot in range(ids.shape[1]):
                here = slice(slot, slot + 1)
                row = row + jnp.where(ids[level, here] == e, gates[level, here], 0.0)
            at = level * experts + e
            mix[at : at + 1] = row
    d = lax.axis_index("dp")
    gains[...] = jnp.zeros_like(gains)
    lane = lax.broadcasted_iota(jnp.int32, (layers, gains.shape[1]), 1)
    inside = (lane >= d * rows) & (lane < (d + 1) * rows)
    for i, gain in enumerate((gain_attn, gain_ffn)):
        wide = jnp.concatenate([gain[...].astype(BF16).astype(F32)] * dp, axis=1)
        gains[i * layers : (i + 1) * layers] = jnp.where(inside, wide, 0.0)
    keeps = []

    def leave(held, target):
        keeps.append(pltpu.make_async_copy(held, target, keep.at[len(keeps)]))
        keeps[-1].start()

    for load in loads_attn:
        load.wait()
    quarter = attn_in[0].shape[2]
    for level in range(layers):
        for i in range(4):
            values = attn_in[i][level]
            values = jnp.transpose(values) if i == 3 else values
            attn_held[level][0, :, i * quarter : (i + 1) * quarter] = values.astype(BF16)
        leave(attn_held[level], attn_out[level])
    for level in range(layers):
        for load in loads_ffn[level]:
            load.wait()
        slim = ffn_in[1].shape[2] // outer
        for group, (held, target) in enumerate(
            ((in_held, in_out), (in_held, in_out), (down_held, down_out))
        ):
            base = (experts + 1) * slim if group == 1 else 0
            for e in range(experts + 1):
                for k in range(outer):
                    cols = slice(k * slim, (k + 1) * slim)
                    if e < experts:
                        values = ffn_in[2 * group][level, e, :, cols]
                    else:
                        values = ffn_in[2 * group + 1][level, :, cols]
                    held[level][k, :, base + e * slim : base + (e + 1) * slim] = values.astype(
                        BF16
                    )
            if group:
                leave(held[level], target[level])
    for copy in keeps:
        copy.wait()


def pack(place, lengths, ids, gates, gain_attn, gain_ffn, attn, ffn, outer, dp):
    dma = pltpu.SemaphoreType.DMA
    layers, rows = gain_attn.shape
    count = place.shape[1]
    width = dp * rows
    experts = ffn[0].shape[1]
    slim = ffn[1].shape[2] // outer
    freqs = (10000.0 ** (-np.arange(HD // 2) / (HD // 2))).astype(np.float32)[:, None]
    blocks = (
        [(1, rows, 4 * attn[0].shape[2])] * layers
        + [(outer, rows, 2 * (experts + 1) * slim)] * layers
        + [(outer, rows, (experts + 1) * slim)] * layers
    )
    return pl.pallas_call(
        functools.partial(pack_kernel, outer, dp),
        out_shape=[
            jax.ShapeDtypeStruct((2, 4, count // 4, 128), F32),
            jax.ShapeDtypeStruct((4, count // 4, 8), F32),
            jax.ShapeDtypeStruct((1, count), F32),
            jax.ShapeDtypeStruct((8, width), F32),
            jax.ShapeDtypeStruct((layers * experts, count), F32),
        ]
        + [jax.ShapeDtypeStruct(block, BF16) for block in blocks],
        in_specs=[VMEM, pl.BlockSpec(memory_space=pltpu.SMEM)] + [VMEM] * 5 + [ANY] * 10,
        out_specs=[VMEM] * 5 + [ANY] * len(blocks),
        scratch_shapes=[pltpu.VMEM(m.shape, F32) for m in attn + ffn]
        + [pltpu.VMEM(block, BF16) for block in blocks]
        + [dma((4,)), dma((layers, 6)), dma((len(blocks),))],
        compiler_params=pltpu.CompilerParams(vmem_limit_bytes=62 << 20),
        name="pack",
    )(place, lengths, jnp.asarray(freqs), ids, gates, gain_attn, gain_ffn, *attn, *ffn)


def unpack_kernel(outer, layers, experts, *refs):
    cut = Cut(refs)
    in_any, down_any, attn_any = cut(layers), cut(layers), cut(layers)
    attn_out, ffn_out = cut(4), cut(6)
    in_v, down_v, attn_v = cut(layers), cut(layers), cut(layers)
    attn_held, ffn_held = cut(4), cut(6)
    load_sem, keep_attn, keep_ffn = cut(3)
    loads = [
        [
            pltpu.make_async_copy(source[level], target[level], load_sem.at[level, i])
            for i, (source, target) in enumerate(
                ((in_any, in_v), (down_any, down_v), (attn_any, attn_v))
            )
        ]
        for level in range(layers)
    ]
    for level in reversed(range(layers)):
        for load in loads[level]:
            load.start()
    keeps = []

    def leave(held, target, sem):
        keeps.append(pltpu.make_async_copy(held, target, sem))
        keeps[-1].start()

    slim = ffn_held[1].shape[2] // outer
    quarter = attn_held[0].shape[2]
    for level in reversed(range(layers)):
        for load in loads[level]:
            load.wait()
        for group, source in enumerate((in_v, in_v, down_v)):
            base = (experts + 1) * slim if group == 1 else 0
            for e in range(experts + 1):
                for k in range(outer):
                    cols = slice(k * slim, (k + 1) * slim)
                    values = source[level][k, :, base + e * slim : base + (e + 1) * slim]
                    if e < experts:
                        ffn_held[2 * group][level, e, :, cols] = values.astype(F32)
                    else:
                        ffn_held[2 * group + 1][level, :, cols] = values.astype(F32)
            for i in (2 * group, 2 * group + 1):
                leave(ffn_held[i].at[level], ffn_out[i].at[level], keep_ffn.at[level, i])
        total = jnp.sum(attn_v[level][...].astype(F32), axis=0)
        for i in range(4):
            values = total[:, i * quarter : (i + 1) * quarter]
            attn_held[i][level] = jnp.transpose(values) if i == 3 else values
            leave(attn_held[i].at[level], attn_out[i].at[level], keep_attn.at[level, i])
    for copy in keeps:
        copy.wait()


def unpack(pushed_in, pushed_down, pushed_attn, experts):
    dma = pltpu.SemaphoreType.DMA
    layers = len(pushed_in)
    outer, rows, third = pushed_down[0].shape
    full = outer * third // (experts + 1)
    quarter = pushed_attn[0].shape[2] // 4
    many, one = (layers, experts, rows, full), (layers, rows, full)
    shapes = [(layers, rows, quarter)] * 3 + [(layers, quarter, rows)] + [many, one] * 3
    moved = pushed_in + pushed_down + pushed_attn
    return pl.pallas_call(
        functools.partial(unpack_kernel, outer, layers, experts),
        out_shape=[jax.ShapeDtypeStruct(shape, F32) for shape in shapes],
        in_specs=[ANY] * len(moved),
        out_specs=[ANY] * 10,
        scratch_shapes=[pltpu.VMEM(part.shape, BF16) for part in moved]
        + [pltpu.VMEM(shape, F32) for shape in shapes]
        + [dma((layers, 3)), dma((layers, 4)), dma((layers, 6))],
        compiler_params=pltpu.CompilerParams(vmem_limit_bytes=62 << 20),
        name="unpack",
    )(*moved)


def layout(place_row, length_row):
    ends = jnp.cumsum(length_row, dtype=jnp.int32)
    after = place_row[:, None] >= ends[None, :]
    begins = jnp.sum(jnp.where(after, length_row[None, :], 0), axis=1, dtype=jnp.int32)
    return place_row - begins


def rope_tables(position):
    half_width = HD // 2
    freqs = 10000.0 ** (-jnp.arange(half_width, dtype=F32) / half_width)
    angles = position.astype(F32)[:, None] * freqs[None, :]
    cosine, sine = jnp.cos(angles), jnp.sin(angles)
    return jnp.stack(
        [
            jnp.concatenate([cosine] * 4, axis=1),
            jnp.concatenate([-sine, sine, -sine, sine], axis=1),
        ]
    )


def norm_back(grad_normed, gain_row, unit_rows, inverse):
    scaled = grad_normed * gain_row
    return inverse * (scaled - unit_rows * jnp.mean(scaled * unit_rows, axis=-1, keepdims=True))


def dot(left, right):
    return jnp.dot(left, right, preferred_element_type=F32)


def dot_nt(left, right):
    return lax.dot_general(left, right, (((1,), (1,)), ((), ())), preferred_element_type=F32)


def dot_tn(left, right):
    return lax.dot_general(left, right, (((0,), (0,)), ((), ())), preferred_element_type=F32)


def make_body(dp):
    outer, inner = split_dp(dp)

    def body(
        tokens,
        place,
        lengths,
        expert_ids,
        gate_values,
        cotangent,
        gain_attn,
        w_query,
        w_key,
        w_value,
        w_out,
        gain_ffn,
        exp_gate,
        exp_up,
        exp_down,
        dense_gate,
        dense_up,
        dense_down,
    ):
        layers, experts, rows, full = exp_gate.shape
        width = tokens.shape[1]
        slim = full // outer
        count = place.shape[1]
        kinds = experts + 1
        merged = rows % 16 == 0
        ids, gates = jnp.swapaxes(expert_ids, 1, 2), jnp.swapaxes(gate_values, 1, 2)
        downs = [jnp.swapaxes(exp_down, 2, 3), jnp.swapaxes(dense_down, 1, 2)]
        ffn = [exp_gate, dense_gate, exp_up, dense_up] + downs
        if merged:
            attn = [w_query, w_key, w_value, w_out]
            tables, marks, spot, gains_own, mix_own, *blocks = pack(
                place, lengths, ids, gates, gain_attn, gain_ffn, attn, ffn, outer, dp
            )
            attn_own = blocks[:layers]
            ffn_own = list(zip(blocks[layers : 2 * layers], blocks[2 * layers :]))
        else:
            position = layout(place[0], lengths[0])
            place_row = place[0].astype(F32)
            marks = jnp.stack([place_row, place_row - position.astype(F32)] * 4, axis=1)
            marks = marks.reshape(4, count // 4, 8)
            spot = place_row[None]
            tables = rope_tables(position).reshape(2, 4, count // 4, 128)
            slots = ids[:, None] == jnp.arange(experts, dtype=jnp.int32)[None, :, None, None]
            mix_own = jnp.sum(jnp.where(slots, gates[:, None], 0.0), axis=2)
            mix_own = mix_own.reshape(layers * experts, count)
            gains_own = jnp.concatenate([gain_attn, gain_ffn], axis=0).astype(BF16).astype(F32)
            spots = jnp.arange(dp, dtype=jnp.int32) == lax.axis_index("dp")
            gains_own = jnp.where(spots[None, :, None], gains_own[:, None], 0.0)
            gains_own = jnp.pad(
                gains_own.reshape(2 * layers, width), ((0, 8 - 2 * layers), (0, 0))
            )
            attn_own, ffn_own = [], []
            for level in range(layers):
                mats = [w_query[level], w_key[level], w_value[level], jnp.transpose(w_out[level])]
                attn_own.append(jnp.concatenate(mats, axis=1).astype(BF16)[None])
                mats = []
                for many, one in ((0, 1), (2, 3), (4, 5)):
                    mats += [ffn[many][level, e] for e in range(experts)] + [ffn[one][level]]
                mats = [m.astype(BF16) for m in mats]
                ffn_own.append(
                    [
                        jnp.stack(
                            [
                                jnp.concatenate(
                                    [m[:, k * slim : (k + 1) * slim] for m in group], axis=1
                                )
                                for k in range(outer)
                            ]
                        )
                        for group in (mats[: 2 * kinds], mats[2 * kinds :])
                    ]
                )
        state = tokens
        lead = [gains_own[None], attn_own[0], mix_own[None]]
        if merged:
            state_in = state
            ahead = [ffn_own[1][1]] if layers > 1 else []
            state, *kept = attn_forward(
                state_in,
                None,
                0,
                None,
                tables,
                marks,
                spot,
                lead + list(ffn_own[0]) + ahead,
                [BOTH] * 5 + [OUTER] * len(ahead),
                outer,
                inner,
                0,
            )
            part_down = kept.pop() if ahead else None
            gains, _, first, mix_all, w_in, w_down = kept[-6:]
            kept = kept[:-6]
        else:
            gains_all, first, mix_all = fetch(lead, outer, inner, 8)
            part_down = None
            gains = jnp.sum(gains_all, axis=0)
        w_attn = [first.reshape(width, -1)]
        w_ffn = []
        kept_attn, kept_ffn = [], []
        for level in range(layers):
            if level == 0 and merged:
                before = state_in
            else:
                before = state
                inside = list(ffn_own[level][: 1 if level else 2])
                state, *kept = attn_forward(
                    before,
                    gains,
                    level,
                    w_attn[level],
                    tables,
                    marks,
                    spot,
                    inside,
                    [BOTH] * len(inside),
                    outer,
                    inner,
                    1 if level else 11,
                )
                if level:
                    w_in = kept.pop()
                else:
                    w_down, w_in = kept.pop(), kept.pop()
            kept_attn.append((before, kept))
            w_ffn.append((w_in.reshape(width, -1), w_down.reshape(width, -1)))
            resid = state
            more, modes = [], []
            if level + 1 < layers:
                half = part_down is not None and level == 0
                more = [attn_own[level + 1], part_down if half else ffn_own[level + 1][1]]
                modes = [BOTH, INNER if half else BOTH]
            state, b_in, both, *fetched = ffn_forward(
                resid,
                gains,
                level,
                layers + level,
                kinds,
                mix_all,
                *w_ffn[level],
                more,
                modes,
                outer,
                inner,
                (2 if level == 0 else 12) if more else 3,
            )
            if more:
                w_attn.append(fetched[0].reshape(width, -1))
                w_down = fetched[1]
            kept_ffn.append((resid, b_in, both))
        mixed = state.astype(BF16)

        grad = cotangent
        part_gains = [None] * (2 * layers)
        pushed_in, pushed_down = [None] * layers, [None] * layers
        pushed_attn = [None] * layers
        waiting = []
        for level in reversed(range(layers)):
            resid, b_in, both = kept_ffn[level]
            grad, part_gain, grad_in, grad_down, *moved = ffn_backward(
                grad,
                resid,
                gains,
                level,
                layers + level,
                kinds,
                mix_all,
                *w_ffn[level],
                b_in,
                both,
                waiting,
                outer,
                inner,
                4 if waiting else 5,
            )
            part_gains[layers + level] = part_gain
            if waiting:
                (pushed_attn[level + 1],) = moved
            before, kept = kept_attn[level]
            inside = [grad_in.reshape(dp, rows, -1), grad_down.reshape(dp, rows, -1)]
            others = part_gains[1:] if level == 0 and merged else []
            grad, part_gain, *moved = attn_backward(
                grad,
                before,
                gains,
                level,
                w_attn[level],
                tables,
                marks,
                spot,
                kept,
                others,
                inside,
                outer,
                inner,
                6 if level else 7,
            )
            if level == 0 and merged:
                pushed_in[0], pushed_down[0], pushed_attn[0] = moved
                gain_sum = lax.dynamic_slice_in_dim(
                    part_gain, lax.axis_index("dp") * rows, rows, axis=1
                )
                continue
            part_gains[level] = part_gain
            waiting = [moved[0].reshape(dp, rows, -1)]
            pushed_in[level], pushed_down[level] = moved[1:]
        if not merged:
            stacked = jnp.concatenate(part_gains, axis=0)
            stacked = jnp.pad(stacked, ((0, 8 - 2 * layers), (0, 0)))
            stacked = jnp.transpose(stacked.reshape(8, dp, rows), (1, 0, 2))
            pushed_attn[0], gain_parts = push([waiting[0], stacked], outer, inner, 9)
            gain_part = jnp.sum(gain_parts, axis=0)
            gain_sum = jnp.sum(
                gather(jnp.pad(gain_part, ((0, 0), (0, 128 - rows))), dp, 10)[0], axis=0
            )
        grad_gain_attn = gain_sum[:layers, :rows]
        grad_gain_ffn = gain_sum[layers : 2 * layers, :rows]

        if merged:
            query, key, value, out, gate, gate_d, up, up_d, down, down_d = unpack(
                pushed_in, pushed_down, pushed_attn, experts
            )
        else:
            ups, downs, attns = [], [], []
            for level in range(layers):
                parts = pushed_in[level].reshape(outer, rows, 2 * kinds, slim)
                ups.append(jnp.transpose(parts, (2, 1, 0, 3)).reshape(2 * kinds, rows, full))
                parts = pushed_down[level].reshape(outer, rows, kinds, slim)
                downs.append(jnp.transpose(parts, (2, 1, 0, 3)).reshape(kinds, rows, full))
                attns.append(jnp.sum(pushed_attn[level].astype(F32), axis=0))
            ups, downs = jnp.stack(ups).astype(F32), jnp.stack(downs).astype(F32)
            gate, gate_d = ups[:, :experts], ups[:, experts]
            up, up_d = ups[:, kinds : kinds + experts], ups[:, kinds + experts]
            down, down_d = downs[:, :experts], downs[:, experts]
            query, key, value, out = jnp.split(jnp.stack(attns), 4, axis=2)
            out = jnp.swapaxes(out, 1, 2)
        return (
            mixed,
            grad,
            grad_gain_attn,
            query,
            key,
            value,
            out,
            grad_gain_ffn,
            gate,
            up,
            jnp.swapaxes(down, 2, 3),
            gate_d,
            up_d,
            jnp.swapaxes(down_d, 1, 2),
        )

    return body


def solution(mesh):
    return jax.shard_map(
        make_body(mesh.shape["dp"]),
        mesh=mesh,
        in_specs=(
            P(("dp", "tensor"), None),
            P("dp", None),
            P("dp", None),
            P(None, "dp", None),
            P(None, "dp", None),
            P(("dp", "tensor"), None),
            P(None, "dp"),
            P(None, "dp", "tensor"),
            P(None, "dp", "tensor"),
            P(None, "dp", "tensor"),
            P(None, "tensor", "dp"),
            P(None, "dp"),
            P(None, None, "dp", "tensor"),
            P(None, None, "dp", "tensor"),
            P(None, None, "tensor", "dp"),
            P(None, "dp", "tensor"),
            P(None, "dp", "tensor"),
            P(None, "tensor", "dp"),
        ),
        out_specs=(
            P(("dp", "tensor"), None),
            P(("dp", "tensor"), None),
            P(None, "dp"),
            P(None, "dp", "tensor"),
            P(None, "dp", "tensor"),
            P(None, "dp", "tensor"),
            P(None, "tensor", "dp"),
            P(None, "dp"),
            P(None, None, "dp", "tensor"),
            P(None, None, "dp", "tensor"),
            P(None, None, "tensor", "dp"),
            P(None, "dp", "tensor"),
            P(None, "dp", "tensor"),
            P(None, "tensor", "dp"),
        ),
        check_vma=False,
    )
```

profile of v0, /device:TPU:9, one launch (start us, length us, event | category | flops | bytes accessed | tf_op | source)
XLA Modules:
  0.0 485.6 jit_solution(3380656418788793023)
XLA Ops:
  0.7 6.6 %pack.1 = (f32[2,4,128,128]{3,2,1,0:T(8,128)}, f32[4,128,8]{2,1,0:T(8,128)}, f32[1,512]{1,0:T(1,128)}, f32[8,768]{1,0:T(8,128)}, f32[8,512]{1,0:T(8,128)}, /*ind...) custom-call(s32[1,512]{1,0:T(1,128)} %refs_0_.3, ...), custom_call_target="tpu_custom_call" | custom-call | tf_op jit(solution)/shard_map/pack/pallas_call | solution.py:1358
  7.3 64.4 %attn_forward.2 = (f32[128,768]{1,0:T(8,128)}, bf16[4,128,768]{2,1,0:T(8,128)(2,1)}, bf16[4,128,384]{2,1,0:T(8,128)(2,1)}, bf16[4,128,192]{2,1,0:T(8,128)(2,1)},...) custom-call(bf16[128,768]{1,0:T(8,128)(2,1)} %refs_1_.3, ...), custom_call_target="tpu_custom_call" | custom-call | tf_op jit(solution)/shard_map/attn_forward/pallas_call | solution.py:1023
  71.7 66.8 %ffn_forward.2 = (f32[128,768]{1,0:T(8,128)}, bf16[4,4,128,768]{3,2,1,0:T(8,128)(2,1)}, bf16[4,2,256,1280]{3,2,1,0:T(8,128)(2,1)}, bf16[8,96,768]{2,1,0:T(8,128)(2,1)}, bf16[8,96,640]{2,1,0:T(8,128)(2,1)}) custom-call(f32[128,768]{1,0:T(8,128)} %get-tuple-element.90.refs_0_.refs_1_, f32[8,768]{1,0:T(8,128)} %get-tuple-element.91.refs_1_.refs_4_.refs_2_, ...), custom_call_target="tpu_custom_call" | custom-call | tf_op jit(solution)/shard_map/ffn_forward/pallas_call | solution.py:693
  138.4 33.9 %attn_forward.3 = (f32[128,768]{1,0:T(8,128)}, bf16[4,128,768]{2,1,0:T(8,128)(2,1)}, bf16[4,128,384]{2,1,0:T(8,128)(2,1)}, bf16[4,128,192]{2,1,0:T(8,128)(2,1)},...) custom-call(f32[128,768]{1,0:T(8,128)} %get-tuple-element.97.refs_0_.refs_1_, ...), custom_call_target="tpu_custom_call" | custom-call | tf_op jit(solution)/shard_map/attn_forward/pallas_call | solution.py:1023
  172.3 69.9 %ffn_forward.3 = (f32[128,768]{1,0:T(8,128)}, bf16[4,4,128,768]{3,2,1,0:T(8,128)(2,1)}, bf16[4,2,256,1280]{3,2,1,0:T(8,128)(2,1)}) custom-call(f32[128,768]{1,0:T(8,128)} %get-tuple-element.100.refs_0_.refs_1_, f32[8,768]{1,0:T(8,128)} %get-tuple-element.91.refs_1_.refs_4_.refs_2_, f32[8,8,512]{2,1,0:T(8,128)} %get-tuple-element.92.refs_2_.refs_3_, ...), custom_call_target="tpu_custom_call" | custom-call | tf_op jit(solution)/shard_map/ffn_forward/pallas_call | solution.py:693
  242.2 1.7 convert_element_type.3
  243.9 55.5 %ffn_backward.2 = (f32[128,768]{1,0:T(8,128)}, f32[1,768]{1,0:T(1,128)}, bf16[768,1280]{1,0:T(8,128)(2,1)}, bf16[768,640]{1,0:T(8,128)(2,1)}) custom-call(bf16[128,768]{1,0:T(8,128)(2,1)} %refs_0_.5, f32[128,768]{1,0:T(8,128)} %get-tuple-element.100.refs_0_.refs_1_, f32[8,768]{1,0:T(8,128)} %get-tuple-element.91.refs_1_.refs_4_.refs_2_, ...), custom_call_target="tpu_custom_call" | custom-call | tf_op jit(solution)/shard_map/ffn_backward/pallas_call | solution.py:836
  299.4 48.0 %attn_backward.2 = (f32[128,768]{1,0:T(8,128)}, f32[1,768]{1,0:T(1,128)}, bf16[768,768]{1,0:T(8,128)(2,1)}, bf16[4,96,1280]{2,1,0:T(8,128)(2,1)}, bf16[4,96,640]{2,1,0:T(8,128)(2,1)}) custom-call(f32[128,768]{1,0:T(8,128)} %get-tuple-element.106.refs_0_, f32[128,768]{1,0:T(8,128)} %get-tuple-element.97.refs_0_.refs_1_, ...), custom_call_target="tpu_custom_call" | custom-call | tf_op jit(solution)/shard_map/attn_backward/pallas_call | solution.py:1204
  347.4 65.5 %ffn_backward.3 = (f32[128,768]{1,0:T(8,128)}, f32[1,768]{1,0:T(1,128)}, bf16[768,1280]{1,0:T(8,128)(2,1)}, bf16[768,640]{1,0:T(8,128)(2,1)}, bf16[4,96,768]{2,1,0:T(8,128)(2,1)}) custom-call(f32[128,768]{1,0:T(8,128)} %get-tuple-element.114.refs_0_, f32[128,768]{1,0:T(8,128)} %get-tuple-element.90.refs_0_.refs_1_, ...), custom_call_target="tpu_custom_call" | custom-call | tf_op jit(solution)/shard_map/ffn_backward/pallas_call | solution.py:836
  412.9 65.6 %attn_backward.3 = (f32[128,768]{1,0:T(8,128)}, f32[8,768]{1,0:T(8,128)}, bf16[4,96,1280]{2,1,0:T(8,128)(2,1)}, bf16[4,96,640]{2,1,0:T(8,128)(2,1)}, bf16[4,96,768]{2,1,0:T(8,128)(2,1)}) custom-call(f32[128,768]{1,0:T(8,128)} %get-tuple-element.118.refs_0_, bf16[128,768]{1,0:T(8,128)(2,1)} %refs_1_.3, f32[8,768]{1,0:T(8,128)} %get-tuple-element.91.refs_1_.refs_4_.refs_2_, ...), custom_call_target="tpu_custom_call" | custom-call | tf_op jit(solution)/shard_map/attn_backward/pallas_call | solution.py:1204
  478.6 0.8 constant_dynamic-slice_fusion
  479.3 0.6 fusion
  479.9 0.0 copy-start
  479.9 4.7 unpack.1
  484.6 0.0 copy-done
  484.6 0.7 copy.34
Async XLA Ops:
  479.9 4.7 copy-start
where the time goes:
time: 489 us; the launch traced here: 486 us
  Pallas kernels  481 us (98%)
    pallas_call x2, Pallas kernels, ffn_forward(): pl.pallas_call(functools.partial(ffn_forward_kernel, outer, inner, kinds,...  137 us
    pallas_call x2, Pallas kernels, ffn_backward(): pl.pallas_call(functools.partial(ffn_backward_kernel, outer, inner, kinds...  121 us
    pallas_call x2, Pallas kernels, attn_backward(): pl.pallas_call(functools.partial(attn_backward_kernel, outer, inner, coun...  114 us
    pallas_call x2, Pallas kernels, attn_forward(): pl.pallas_call(functools.partial(attn_forward_kernel, outer, inner, modes...  98.2 us

commit v1 on v0

--- a/solution.py
+++ b/solution.py
@@ -187,10 +187,17 @@
         for step in range(self.parts):
             self.forward(step)
 
+    def hop(self, step):
+        ((inside, copy),) = self.passes(step)
+
+        @pl.when(inside)
+        def _():
+            copy.wait_recv()
+            copy.start()
+
     def arrive(self, step):
-        self.outward(step, self.dz, None).wait_recv()
-        for inside, copy in self.passes(step):
-            pl.when(inside)(copy.start)
+        ((inside, copy),) = self.passes(step)
+        pl.when(jnp.logical_not(inside))(copy.wait_recv)
         self.forward(step)
 
     def forward(self, step):
@@ -217,7 +224,7 @@
 class Scatter:
     def __init__(self, outer, inner, part, room, sems, parts=1):
         self.outer, self.part, self.parts = outer, part, parts
-        self.from_c, self.sum_c, self.from_y, self.sum_y, self.from_z = room
+        self.from_c, self.from_y, self.from_z = room
         self.cs, self.cr, self.ys, self.yr, self.zs, self.zr = sems
         dz, dx, t = place_of(inner)
         d = lax.axis_index("dp")
@@ -247,9 +254,9 @@
         source = self.source[step // self.parts]
         self.cc[step].wait_recv()
         mine = self.part[source, :, self.c, self.rows(step)].astype(F32)
-        self.sum_c[step] = (mine + self.from_c[step].astype(F32)).astype(BF16)
+        self.from_c[step] = (mine + self.from_c[step].astype(F32)).astype(BF16)
         self.yc[step] = send(
-            self.sum_c.at[step, 1 - self.y],
+            self.from_c.at[step, 1 - self.y],
             self.from_y.at[step],
             self.ys.at[step],
             self.yr.at[step],
@@ -258,7 +265,7 @@
 
     def summed(self, step):
         self.yc[step].wait_recv()
-        return self.sum_c[step, self.y].astype(F32) + self.from_y[step].astype(F32)
+        return self.from_c[step, self.y].astype(F32) + self.from_y[step].astype(F32)
 
     def outward(self, step, source, away):
         at = (away - 1) * self.parts + step % self.parts
@@ -272,9 +279,9 @@
         )
 
     def outer_send(self, step):
-        self.sum_y[step] = self.summed(step).astype(BF16)
+        self.from_y[step] = self.summed(step).astype(BF16)
         away = lax.rem(self.source[step // self.parts] - self.dz + self.outer, self.outer)
-        self.zc[step] = self.outward(step, self.sum_y.at[step], away)
+        self.zc[step] = self.outward(step, self.from_y.at[step], away)
         self.zc[step].start()
 
     def total(self):
@@ -283,7 +290,7 @@
             total = self.summed(piece)
             for step in range(self.parts + piece, self.steps, self.parts):
                 away = lax.rem(self.dz - self.source[step // self.parts] + self.outer, self.outer)
-                self.outward(step, self.sum_y.at[step], away).wait_recv()
+                self.outward(step, self.from_y.at[step], away).wait_recv()
                 at = (away - 1) * self.parts + piece
                 total = total + self.from_z[at].astype(F32)
             pieces.append(total)
@@ -310,51 +317,63 @@
     steps, size = outer * parts, rows // parts
     return [
         pltpu.VMEM((steps, 2, size, width), BF16),
-        pltpu.VMEM((steps, 2, size, width), BF16),
-        pltpu.VMEM((steps, size, width), BF16),
         pltpu.VMEM((steps, size, width), BF16),
         pltpu.VMEM((max(steps - parts, 1), size, width), BF16),
     ]
 
 
-def pipeline(take, give, compute, begin, after, middle, late):
+def pipeline(take, give, compute, begin, after, post, middle, since, late):
     steps, parts = take.steps, take.parts
     middle, late = list(middle), list(late)
     lag = parts + 1
     take.start()
     begin()
+    hops = list(range(parts, steps))
+    for _ in range(min(2 * parts, len(hops))):
+        take.hop(hops.pop(0))
     for step in range(steps):
         if step + parts < steps:
             take.arrive(step + parts)
-        if step + parts == steps - 1:
-            after()
         take.complete(step)
         compute(step)
         give.core_send(step)
+        for _ in range(min(parts, len(hops))):
+            take.hop(hops.pop(0))
         if step:
             give.pair_send(step - 1)
         if step - lag >= parts:
             give.outer_send(step - lag)
-        if step + parts >= steps and middle:
+        if step == 1:
+            after()
+        if step >= since and middle:
             middle.pop(0)()
+        post(step)
     sent = max(parts, steps - lag)
     late = middle + late
-    share = max(1, (len(late) + lag) // (lag + 1))
     give.pair_send(steps - 1)
     for step in range(sent, steps):
-        for _ in range(share):
-            if late:
-                late.pop(0)()
+        if late:
+            late.pop(0)()
         give.outer_send(step)
     for work in late:
         work()
+
+
+def pieces_of(arrays, halves=True):
+    items = []
+    for i, array in enumerate(arrays):
+        wide = array.shape[-1]
+        count = 2 if halves and wide % 256 == 0 and wide > 1024 else 1
+        size = wide // count
+        items += [(i, slice(at * size, (at + 1) * size)) for at in range(count)]
+    return items
 
 
 class Fetch:
     def __init__(self, outer, inner, owns, outs, holds, sems, modes):
         self.outer, self.inner, self.owns, self.outs, self.holds = outer, inner, owns, outs, holds
         self.zs, self.zr, self.xs, self.xr, self.ls = sems
-        self.modes = modes
+        self.modes, self.items = modes, pieces_of(owns)
         self.dz, dx, t = place_of(inner)
         self.dx, self.d = dx, lax.axis_index("dp")
         self.source = [nearest(self.dz, outer, step) for step in range(outer)]
@@ -362,20 +381,28 @@
         self.xdev = [(self.dz * inner + lax.rem(dx + j, inner), t) for j in range(1, inner)]
         self.zc, self.xc, self.into, self.back = [], {}, {}, {}
 
-    def own(self, i, where):
-        return self.owns[i].at[where if self.owns[i].shape[0] == self.outer else 0]
-
-    def slot(self, i, source):
-        if self.modes[i] == OUTER:
-            return self.outs[i].at[source]
-        return self.outs[i].at[source * self.inner + self.dx]
-
-    def copy(self, i, step, source, target):
-        away = lax.rem(source + self.outer, self.outer)
-        at = i * self.outer + away
+    def own(self, item, where):
+        i, cols = self.items[item]
+        return self.owns[i].at[where if self.owns[i].shape[0] == self.outer else 0, :, cols]
+
+    def slot(self, item, source):
+        i, cols = self.items[item]
+        if self.modes[i] != OUTER:
+            source = source * self.inner + self.dx
+        return self.outs[i].at[source, :, cols]
+
+    def mode(self, item):
+        return self.modes[self.items[item][0]]
+
+    def chosen(self, first, last):
+        last = len(self.owns) if last is None else last
+        return [item for item, (i, _) in enumerate(self.items) if first <= i < last]
+
+    def copy(self, item, step, away, refs):
+        at = item * self.outer + lax.rem(away + self.outer, self.outer)
         return pltpu.make_async_remote_copy(
-            src_ref=target[0],
-            dst_ref=target[1],
+            src_ref=refs[0],
+            dst_ref=refs[1],
             send_sem=self.zs.at[at],
             recv_sem=self.zr.at[at],
             device_id=self.zdev[step],
@@ -383,32 +410,35 @@
         )
 
     def start(self, first=0, last=None, aside=True):
+        for item in self.chosen(first, last):
+            i, cols = self.items[item]
+            if self.mode(item) == INNER:
+                for step, source in enumerate(self.source):
+                    here = self.owns[i].at[source, :, cols]
+                    self.spread(item, step, here, self.slot(item, source))
+                continue
+            for step in range(1, self.outer):
+                source = self.source[step]
+                refs = (self.own(item, source), self.slot(item, self.dz))
+                self.zc.append(self.copy(item, step, source - self.dz, refs))
+                self.zc[-1].start()
+            if aside:
+                self.aside(item)
         for i in range(first, len(self.owns) if last is None else last):
-            inner = self.modes[i] == INNER
-            here = self.owns[i] if inner else self.own(i, self.dz)
+            where = self.dz if self.owns[i].shape[0] == self.outer else 0
+            here = self.owns[i] if self.modes[i] == INNER else self.owns[i].at[where]
             at = i * (self.outer + 1)
             self.into[i] = pltpu.make_async_copy(here, self.holds[i], self.ls.at[at])
             self.into[i].start()
-            if inner:
-                for step, source in enumerate(self.source):
-                    self.spread(i, step, self.owns[i].at[source], self.slot(i, source))
-                continue
-            for step in range(1, self.outer):
-                source = self.source[step]
-                refs = (self.own(i, source), self.slot(i, self.dz))
-                self.zc.append(self.copy(i, step, source - self.dz, refs))
-                self.zc[-1].start()
-            if aside:
-                self.aside(i)
-
-    def aside(self, i):
-        if self.modes[i] == BOTH:
-            self.spread(i, 0, self.own(i, self.dz), self.slot(i, self.dz))
-
-    def spread(self, i, step, block, target):
+
+    def aside(self, item):
+        if self.mode(item) == BOTH:
+            self.spread(item, 0, self.own(item, self.dz), self.slot(item, self.dz))
+
+    def spread(self, item, step, block, target):
         for j in range(1, self.inner):
-            at = (i * self.outer + step) * self.inner + j
-            self.xc[i, step, j] = send(
+            at = (item * self.outer + step) * self.inner + j
+            self.xc[item, step, j] = send(
                 block, target, self.xs.at[at], self.xr.at[at], self.xdev[j - 1]
             )
 
@@ -416,12 +446,15 @@
         for i, into in self.into.items():
             into.wait()
             at = i * (self.outer + 1)
+            target = self.outs[i]
             if self.modes[i] == INNER:
                 pairs = [
-                    (self.holds[i].at[source], self.slot(i, source)) for source in self.source
+                    (self.holds[i].at[source], target.at[source * self.inner + self.dx])
+                    for source in self.source
                 ]
             else:
-                pairs = [(self.holds[i], self.slot(i, self.dz))]
+                here = self.dz if self.modes[i] == OUTER else self.d
+                pairs = [(self.holds[i], target.at[here])]
             self.back[i] = [
                 pltpu.make_async_copy(*pair, self.ls.at[at + 1 + k])
                 for k, pair in enumerate(pairs)
@@ -429,31 +462,31 @@
             for copy in self.back[i]:
                 copy.start()
 
-    def turn(self, i, step):
+    def turn(self, item, step):
         source = self.source[step]
-        block = self.slot(i, source)
-        self.copy(i, step, self.dz - source, (block, block)).wait_recv()
-        if self.modes[i] == BOTH:
-            self.spread(i, step, block, block)
+        block = self.slot(item, source)
+        self.copy(item, step, self.dz - source, (block, block)).wait_recv()
+        if self.mode(item) == BOTH:
+            self.spread(item, step, block, block)
 
     def turns(self, first=0, last=None):
         return [
-            functools.partial(self.turn, i, step)
-            for i in range(first, len(self.owns) if last is None else last)
+            functools.partial(self.turn, item, step)
+            for item in self.chosen(first, last)
             for step in range(1, self.outer)
-            if self.modes[i] != INNER
+            if self.mode(item) != INNER
         ]
 
     def land(self, i):
         for key in self.xc:
-            if key[0] == i:
+            if self.items[key[0]][0] == i:
                 self.xc[key].wait_recv()
         for copy in self.back[i]:
             copy.wait()
 
     def finish(self, first=0):
         for key in self.xc:
-            if key[0] >= first:
+            if self.items[key[0]][0] >= first:
                 self.xc[key].wait_recv()
             self.xc[key].wait_send()
         for copy in self.zc:
@@ -475,7 +508,7 @@
 
 def fetch_scratch(owns, outer, inner, modes):
     dma = pltpu.SemaphoreType.DMA
-    count = max(len(owns), 1)
+    count = max(len(pieces_of(owns)), 1)
     return [
         pltpu.VMEM(own.shape if mode == INNER else own.shape[1:], own.dtype)
         for own, mode in zip(owns, modes)
@@ -484,14 +517,15 @@
         dma((count * outer,)),
         dma((count * outer * inner,)),
         dma((count * outer * inner,)),
-        dma((count * (outer + 1),)),
+        dma((max(len(owns), 1) * (outer + 1),)),
     ]
 
 
 class Push:
-    def __init__(self, outer, inner, parts, outs, room, sems):
+    def __init__(self, outer, inner, parts, outs, room, sems, halves=True):
         count = len(parts)
         self.outer, self.inner, self.parts, self.outs = outer, inner, parts, outs
+        self.items = pieces_of(parts, halves)
         self.froms, self.mine, self.sums = room[:count], room[count : 2 * count], room[2 * count :]
         self.xs, self.xr, self.zs, self.zr, self.ls, self.ks = sems
         self.dz, dx, t = place_of(inner)
@@ -503,49 +537,50 @@
         self.xc, self.zc, self.loads, self.keeps = {}, [], {}, []
 
     def start(self, first=0, last=None):
-        for i in range(first, len(self.parts) if last is None else last):
+        last = len(self.parts) if last is None else last
+        for item, (i, cols) in enumerate(self.items):
+            if not first <= i < last:
+                continue
             for step, source in enumerate(self.source):
                 for j in range(1, self.inner):
                     slot = source * self.inner + lax.rem(self.dx + j, self.inner)
-                    at = (i * self.outer + step) * self.inner + j
-                    self.xc[i, step, j] = send(
-                        self.parts[i].at[slot],
-                        self.froms[i].at[j - 1, step],
+                    at = (item * self.outer + step) * self.inner + j
+                    self.xc[item, step, j] = send(
+                        self.parts[i].at[slot, :, cols],
+                        self.froms[i].at[j - 1, step, :, cols],
                         self.xs.at[at],
                         self.xr.at[at],
                         self.xdev[j - 1],
                     )
-                self.loads[i, step] = pltpu.make_async_copy(
-                    self.parts[i].at[source * self.inner + self.dx],
-                    self.mine[i].at[step],
-                    self.ls.at[i * self.outer + step],
+                self.loads[item, step] = pltpu.make_async_copy(
+                    self.parts[i].at[source * self.inner + self.dx, :, cols],
+                    self.mine[i].at[step, :, cols],
+                    self.ls.at[item * self.outer + step],
                 )
-                self.loads[i, step].start()
-
-    def turn(self, i, step):
-        self.loads[i, step].wait()
-        total = self.mine[i][step].astype(F32)
+                self.loads[item, step].start()
+
+    def turn(self, item, step):
+        i, cols = self.items[item]
+        self.loads[item, step].wait()
+        total = self.mine[i][step, :, cols].astype(F32)
         for j in range(1, self.inner):
-            self.xc[i, step, j].wait_recv()
-            total = total + self.froms[i][j - 1, step].astype(F32)
-        self.sums[i][step] = total.astype(self.sums[i].dtype)
-        target = self.outs[i].at[self.dz]
+            self.xc[item, step, j].wait_recv()
+            total = total + self.froms[i][j - 1, step, :, cols].astype(F32)
+        self.sums[i][step, :, cols] = total.astype(self.sums[i].dtype)
+        source = self.sums[i].at[step, :, cols]
+        target = self.outs[i].at[self.dz, :, cols]
         if step < self.outer - 1:
             away = lax.rem(self.source[step] - self.dz + self.outer, self.outer)
-            at = i * self.outer + away
-            self.zc.append(
-                send(self.sums[i].at[step], target, self.zs.at[at], self.zr.at[at], self.zdev[step])
-            )
+            at = item * self.outer + away
+            self.zc.append(send(source, target, self.zs.at[at], self.zr.at[at], self.zdev[step]))
         else:
-            self.keeps.append(
-                pltpu.make_async_copy(self.sums[i].at[step], target, self.ks.at[i])
-            )
+            self.keeps.append(pltpu.make_async_copy(source, target, self.ks.at[item]))
             self.keeps[-1].start()
 
     def turns(self):
         return [
-            functools.partial(self.turn, i, step)
-            for i in range(len(self.parts))
+            functools.partial(self.turn, item, step)
+            for item in range(len(self.items))
             for step in range(self.outer)
         ]
 
@@ -565,7 +600,7 @@
 
 def push_scratch(parts, outer, inner):
     dma = pltpu.SemaphoreType.DMA
-    count = max(len(parts), 1)
+    count = max(len(pieces_of(parts)), 1)
     across_x = [pltpu.VMEM((inner - 1, outer) + part.shape[1:], part.dtype) for part in parts]
     own = [pltpu.VMEM((outer,) + part.shape[1:], part.dtype) for part in parts]
     return (
@@ -616,8 +651,8 @@
     owns = cut(count)
     out, b_out, gu_out = cut(3)
     fetched = cut(count)
-    w_in, w_down, b, gu, part, mix_rows, mix = cut(7)
-    room, take_sems, give_sems = cut(5), cut(6), cut(6)
+    w_in, w_down, b, gu, hid, part, mix_rows, mix = cut(8)
+    room, take_sems, give_sems = cut(3), cut(6), cut(6)
     load_sem, keep_b, keep_gu, load_mix = cut(4)
     extra = Fetch(outer, inner, owns, fetched, cut(count), cut(5), modes) if count else None
     rows, width = resid.shape
@@ -646,21 +681,25 @@
             for load in loads:
                 load.wait()
         rows_in = b[source, :, here].reshape(4 * size, width)
+
         scale = mix[source, :, here].reshape(4 * size, mix.shape[-1])
         both = dot(rows_in, w_in[...])
         gu[source, q] = both.astype(BF16)
         gate, up = both[:, :third], both[:, third:]
         hidden = gate * jax.nn.sigmoid(gate) * up
-        pieces = []
         for e in range(kinds):
             piece = hidden[:, e * slim : (e + 1) * slim]
             if e < kinds - 1:
-                at = level * (kinds - 1) + e
-                piece = piece * scale[:, at : at + 1]
-            pieces.append(piece.astype(BF16))
-        hidden = jnp.concatenate(pieces, axis=1)
-        sent = dot_nt(hidden, w_down[...]).astype(BF16)
-        part[source, :, :, here] = sent.reshape(2, 2, size, width)
+                col = level * (kinds - 1) + e
+                piece = piece * scale[:, col : col + 1]
+            hid[:, e * slim : (e + 1) * slim] = piece.astype(BF16)
+
+        @pl.loop(0, width // 256)
+        def _(at):
+            cols = pl.ds(pl.multiple_of(at * 256, 256), 256)
+            sent = dot_nt(hid[...], w_down[cols]).astype(BF16)
+            part[source, :, :, here, cols] = sent.reshape(2, 2, size, 256)
+
         if q == PARTS - 1:
             at = step // PARTS
             keeps.append(pltpu.make_async_copy(b.at[source], b_out.at[source], keep_b.at[at]))
@@ -673,7 +712,9 @@
             extra.start()
             extra.settle()
 
-    pipeline(take, give, compute, mixer.turn, after, extra.turns() if count else [], [])
+    turns = extra.turns() if count else []
+    half = take.steps // 2
+    pipeline(take, give, compute, mixer.turn, after, lambda step: None, turns, half, [])
     out[...] = resid[...] + give.total()
     take.finish()
     give.finish()
@@ -705,6 +746,7 @@
             pltpu.VMEM(w_down.shape, BF16),
             pltpu.VMEM((outer, 4, rows, width), BF16),
             pltpu.VMEM((outer, PARTS, 4 * rows // PARTS, 2 * third), BF16),
+            pltpu.VMEM((4 * rows // PARTS, third), BF16),
             pltpu.VMEM((outer, 2, 2, rows, width), BF16),
             pltpu.VMEM((outer,) + mix.shape[1:], F32),
             pltpu.VMEM((outer, 4, rows, mix.shape[1]), F32),
@@ -727,8 +769,8 @@
     parts = cut(count)
     out, gain_out, grad_in, grad_down = cut(4)
     pushed = cut(count)
-    w_in, w_down, b, gb, gu, dgu, hid, flip, part, mix_rows, mix = cut(11)
-    room, take_sems, give_sems = cut(5), cut(6), cut(6)
+    w_in, w_down, b, gb, gu, dgu, hid, flip_b, flip_gb, part, mix_rows, mix = cut(12)
+    room, take_sems, give_sems = cut(3), cut(6), cut(6)
     load_sem, load_gu, load_mix = cut(3)
     extra = Push(outer, inner, parts, pushed, cut(3 * count), cut(6)) if count else None
     rows, width = resid.shape
@@ -781,18 +823,23 @@
             hid[source, q, :, cols] = (hidden[:, cols] * scale).astype(BF16)
             dgu[source, q, :, cols] = (grad_gate[:, cols] * scale).astype(BF16)
             dgu[source, q, :, more] = (grad_up[:, cols] * scale).astype(BF16)
-        sent = dot_nt(dgu[source, q], w_in[...]).astype(BF16)
-        part[source, :, :, here] = sent.reshape(2, 2, size, width)
-
-    def turned(table):
-        @pl.loop(0, outer)
-        def _(source):
-            for q in range(PARTS):
-                block = table[source, :, q * size : (q + 1) * size].reshape(4 * size, width)
-                at = pl.multiple_of((source * PARTS + q) * 4 * size, 4 * size)
-                flip[:, pl.ds(at, 4 * size)] = jnp.transpose(block)
-
-    def weigh(target, source, low, high):
+
+        @pl.loop(0, width // 256)
+        def _(at):
+            cols = pl.ds(pl.multiple_of(at * 256, 256), 256)
+            sent = dot_nt(dgu[source, q], w_in[cols]).astype(BF16)
+            part[source, :, :, here, cols] = sent.reshape(2, 2, size, 256)
+
+    def post(step):
+        source, q = take.origin(step), step % PARTS
+        if step == 0:
+            loads[0].wait()
+        at = pl.multiple_of((source * PARTS + q) * 4 * size, 4 * size)
+        for table, flip in ((b, flip_b), (gb, flip_gb)):
+            block = table[source, :, take.rows(step)].reshape(4 * size, width)
+            flip[:, pl.ds(at, 4 * size)] = jnp.transpose(block)
+
+    def weigh(target, flip, source, low, high):
         values = source[...].reshape(tall, source.shape[-1])
 
         @pl.loop(0, width // 256)
@@ -804,16 +851,14 @@
         if count:
             extra.start()
         mixer.turn()
-        loads[0].wait()
-        turned(b)
 
     def pieces(total):
         return [(low, min(low + 256, total)) for low in range(0, total, 256)]
 
-    late = [functools.partial(weigh, grad_in, dgu, *span) for span in pieces(2 * third)]
-    late += [functools.partial(turned, gb)]
-    late += [functools.partial(weigh, grad_down, hid, *span) for span in pieces(third)]
-    pipeline(take, give, compute, begin, lambda: None, extra.turns() if count else [], late)
+    late = [functools.partial(weigh, grad_in, flip_b, dgu, *span) for span in pieces(2 * third)]
+    late += [functools.partial(weigh, grad_down, flip_gb, hid, *span) for span in pieces(third)]
+    turns = extra.turns() if count else []
+    pipeline(take, give, compute, begin, lambda: None, post, turns, 2, late)
     grad_b = give.total()
     x = resid[...]
     inverse = lax.rsqrt(jnp.mean(x * x, axis=-1, keepdims=True) + EPSILON)
@@ -853,6 +898,7 @@
             pltpu.VMEM((outer, PARTS, 4 * rows // PARTS, 2 * third), BF16),
             pltpu.VMEM((outer, PARTS, 4 * rows // PARTS, third), BF16),
             pltpu.VMEM((width, outer * 4 * rows), BF16),
+            pltpu.VMEM((width, outer * 4 * rows), BF16),
             pltpu.VMEM((outer, 2, 2, rows, width), BF16),
             pltpu.VMEM((outer,) + mix.shape[1:], F32),
             pltpu.VMEM((outer, 4, rows, mix.shape[1]), F32),
@@ -894,7 +940,7 @@
     gain_out = cut(1)[0] if lead else None
     fetched = cut(count)
     w, a, qk, v, att, part = cut(6)
-    room, take_sems, give_sems = cut(5), cut(6), cut(6)
+    room, take_sems, give_sems = cut(3), cut(6), cut(6)
     load_sem, keep_sem = cut(2)
     extra = Fetch(outer, inner, owns, fetched, cut(count), cut(5), modes)
     rows, width = x_in.shape
@@ -924,8 +970,8 @@
         take.start()
         for turn in turns[1:]:
             turn()
-        for i in range(2, count):
-            extra.aside(i)
+        for item in extra.chosen(2, None):
+            extra.aside(item)
         extra.land(1)
         slot = fetched[1].shape[1]
         loads = [
@@ -1063,13 +1109,13 @@
     total = count + 1 if last else count
     pushed = cut(total)
     w, a, qk, v, att, ga, g_att, raw, part = cut(9)
-    room, take_sems, give_sems = cut(5), cut(6), cut(6)
+    room, take_sems, give_sems = cut(3), cut(6), cut(6)
     (load_sem,) = cut(1)
     room_x, sems_x = cut(3 * total), cut(6)
     if last:
         held, from_t, from_d, ts, tr, ds, dr = cut(7)
         parts = tuple(parts) + (held,)
-    extra = Push(outer, inner, parts, pushed, room_x, sems_x)
+    extra = Push(outer, inner, parts, pushed, room_x, sems_x, not last)
     turns = extra.turns()
     friends = []
     rows, width = x_in.shape

time: 489 us -> 471 us (0.963)
  Pallas kernels: 481 us -> 460 us
    pallas_call x2, Pallas kernels: 137 us -> 118 us  [ffn_forward(): pl.pallas_call(functools.partial(ffn_forward_kernel, outer, inner, kinds,...]
    pallas_call x2, Pallas kernels: 121 us -> 115 us  [ffn_backward(): pl.pallas_call(functools.partial(ffn_backward_kernel, outer, inner, kinds...]
where the time goes in v1:
time: 471 us; the launch traced here: 464 us
  Pallas kernels  460 us (98%)
    pallas_call x2, Pallas kernels, ffn_forward(): pl.pallas_call(functools.partial(ffn_forward_kernel, outer, inner, kinds,...  118 us
    pallas_call x2, Pallas kernels, ffn_backward(): pl.pallas_call(functools.partial(ffn_backward_kernel, outer, inner, kinds...  115 us
    pallas_call x2, Pallas kernels, attn_backward(): pl.pallas_call(functools.partial(attn_backward_kernel, outer, inner, coun...  113 us
    pallas_call x2, Pallas kernels, attn_forward(): pl.pallas_call(functools.partial(attn_forward_kernel, outer, inner, modes...  102 us

profile of v1, /device:TPU:9, one launch (start us, length us, event | category | flops | bytes accessed | tf_op | source)
XLA Modules:
  0.0 464.3 jit_solution(582839300639817062)
XLA Ops:
  0.7 6.6 %pack.1 = (f32[2,4,128,128]{3,2,1,0:T(8,128)}, f32[4,128,8]{2,1,0:T(8,128)}, f32[1,512]{1,0:T(1,128)}, f32[8,768]{1,0:T(8,128)}, f32[8,512]{1,0:T(8,128)}, /*ind...) custom-call(s32[1,512]{1,0:T(1,128)} %refs_0_.3, ...), custom_call_target="tpu_custom_call" | custom-call | tf_op jit(solution)/shard_map/pack/pallas_call | solution.py:1404
  7.3 65.8 %attn_forward.2 = (f32[128,768]{1,0:T(8,128)}, bf16[4,128,768]{2,1,0:T(8,128)(2,1)}, bf16[4,128,384]{2,1,0:T(8,128)(2,1)}, bf16[4,128,192]{2,1,0:T(8,128)(2,1)},...) custom-call(bf16[128,768]{1,0:T(8,128)(2,1)} %refs_1_.3, ...), custom_call_target="tpu_custom_call" | custom-call | tf_op jit(solution)/shard_map/attn_forward/pallas_call | solution.py:1069
  73.1 62.7 %ffn_forward.2 = (f32[128,768]{1,0:T(8,128)}, bf16[4,4,128,768]{3,2,1,0:T(8,128)(2,1)}, bf16[4,2,256,1280]{3,2,1,0:T(8,128)(2,1)}, bf16[8,96,768]{2,1,0:T(8,128)(2,1)}, bf16[8,96,640]{2,1,0:T(8,128)(2,1)}) custom-call(f32[128,768]{1,0:T(8,128)} %get-tuple-element.90.refs_0_.refs_1_, f32[8,768]{1,0:T(8,128)} %get-tuple-element.91.refs_1_.refs_4_.refs_2_, ...), custom_call_target="tpu_custom_call" | custom-call | tf_op jit(solution)/shard_map/ffn_forward/pallas_call | solution.py:734
  135.8 36.0 %attn_forward.3 = (f32[128,768]{1,0:T(8,128)}, bf16[4,128,768]{2,1,0:T(8,128)(2,1)}, bf16[4,128,384]{2,1,0:T(8,128)(2,1)}, bf16[4,128,192]{2,1,0:T(8,128)(2,1)},...) custom-call(f32[128,768]{1,0:T(8,128)} %get-tuple-element.97.refs_0_.refs_1_, ...), custom_call_target="tpu_custom_call" | custom-call | tf_op jit(solution)/shard_map/attn_forward/pallas_call | solution.py:1069
  171.8 55.4 %ffn_forward.3 = (f32[128,768]{1,0:T(8,128)}, bf16[4,4,128,768]{3,2,1,0:T(8,128)(2,1)}, bf16[4,2,256,1280]{3,2,1,0:T(8,128)(2,1)}) custom-call(f32[128,768]{1,0:T(8,128)} %get-tuple-element.100.refs_0_.refs_1_, f32[8,768]{1,0:T(8,128)} %get-tuple-element.91.refs_1_.refs_4_.refs_2_, f32[8,8,512]{2,1,0:T(8,128)} %get-tuple-element.92.refs_2_.refs_3_, ...), custom_call_target="tpu_custom_call" | custom-call | tf_op jit(solution)/shard_map/ffn_forward/pallas_call | solution.py:734
  227.3 1.7 convert_element_type.3
  229.0 58.2 %ffn_backward.2 = (f32[128,768]{1,0:T(8,128)}, f32[1,768]{1,0:T(1,128)}, bf16[768,1280]{1,0:T(8,128)(2,1)}, bf16[768,640]{1,0:T(8,128)(2,1)}) custom-call(bf16[128,768]{1,0:T(8,128)(2,1)} %refs_0_.5, f32[128,768]{1,0:T(8,128)} %get-tuple-element.100.refs_0_.refs_1_, f32[8,768]{1,0:T(8,128)} %get-tuple-element.91.refs_1_.refs_4_.refs_2_, ...), custom_call_target="tpu_custom_call" | custom-call | tf_op jit(solution)/shard_map/ffn_backward/pallas_call | solution.py:881
  287.2 47.4 %attn_backward.2 = (f32[128,768]{1,0:T(8,128)}, f32[1,768]{1,0:T(1,128)}, bf16[768,768]{1,0:T(8,128)(2,1)}, bf16[4,96,1280]{2,1,0:T(8,128)(2,1)}, bf16[4,96,640]{2,1,0:T(8,128)(2,1)}) custom-call(f32[128,768]{1,0:T(8,128)} %get-tuple-element.106.refs_0_, f32[128,768]{1,0:T(8,128)} %get-tuple-element.97.refs_0_.refs_1_, ...), custom_call_target="tpu_custom_call" | custom-call | tf_op jit(solution)/shard_map/attn_backward/pallas_call | solution.py:1250
  334.6 57.1 %ffn_backward.3 = (f32[128,768]{1,0:T(8,128)}, f32[1,768]{1,0:T(1,128)}, bf16[768,1280]{1,0:T(8,128)(2,1)}, bf16[768,640]{1,0:T(8,128)(2,1)}, bf16[4,96,768]{2,1,0:T(8,128)(2,1)}) custom-call(f32[128,768]{1,0:T(8,128)} %get-tuple-element.114.refs_0_, f32[128,768]{1,0:T(8,128)} %get-tuple-element.90.refs_0_.refs_1_, ...), custom_call_target="tpu_custom_call" | custom-call | tf_op jit(solution)/shard_map/ffn_backward/pallas_call | solution.py:881
  391.7 65.6 %attn_backward.3 = (f32[128,768]{1,0:T(8,128)}, f32[8,768]{1,0:T(8,128)}, bf16[4,96,1280]{2,1,0:T(8,128)(2,1)}, bf16[4,96,640]{2,1,0:T(8,128)(2,1)}, bf16[4,96,768]{2,1,0:T(8,128)(2,1)}) custom-call(f32[128,768]{1,0:T(8,128)} %get-tuple-element.118.refs_0_, bf16[128,768]{1,0:T(8,128)(2,1)} %refs_1_.3, f32[8,768]{1,0:T(8,128)} %get-tuple-element.91.refs_1_.refs_4_.refs_2_, ...), custom_call_target="tpu_custom_call" | custom-call | tf_op jit(solution)/shard_map/attn_backward/pallas_call | solution.py:1250
  457.3 0.8 constant_dynamic-slice_fusion
  458.1 0.6 fusion
  458.7 0.0 copy-start
  458.7 4.7 %unpack.1 = (f32[2,96,192]{2,1,0:T(8,128)}, f32[2,96,192]{2,1,0:T(8,128)}, f32[2,96,192]{2,1,0:T(8,128)}, f32[2,192,96]{2,1,0:T(8,128)}, f32[2,4,96,512]{3,2,1,0...) custom-call(bf16[4,96,1280]{2,1,0:T(8,128)(2,1)} %get-tuple-element., ...), custom_call_target="tpu_custom_call" | custom-call | tf_op jit(solution)/shard_map/unpack/pallas_call | solution.py:1484
  463.3 0.0 copy-done
  463.3 0.7 copy.34
Async XLA Ops:
  458.7 4.7 %copy-start = (f32[128,768]{1,0:T(8,128)S(1)}, f32[128,768]{1,0:T(8,128)}, u32[]{:S(2)}) copy-start(f32[128,768]{1,0:T(8,128)} %get-tuple-element.165) | copy-start | bytes 1179652
